TPU v7x, 256 devices: a whole 4x4x8 slice. The times are simulated.
256 devices in a mesh: ctx: 8 (over y, core), vocab: 32 (over x, z).
Axes of the slice: x: 4, y: 4, z: 8, core: 2. Of those that a mesh axis runs over, the one named last changes fastest.
Arguments:
- resid_out: bfloat16 [2048, 4096], P('ctx', 'vocab'), may hold values from -4 to 4
- final_gain: float32 [4096], replicated, may hold values from 0.5 to 1.5
- head_weight: bfloat16 [4096, 32768], P('ctx', 'vocab'), may hold values from -2 to 2
- targets: int32 [2048], P('ctx'), may hold values from 0 to 32767
- out_weight: bfloat16 [8192, 4096], P('vocab', 'ctx'), may hold values from -0.0625 to 0.0625
- norm_gain: float32 [8192], P('vocab'), may hold values from 0.5 to 1.5
- xs: bfloat16 [2048, 8192], P('ctx', 'vocab'), may hold values from -6 to 6
- gate_z: bfloat16 [2048, 8192], P('ctx', 'vocab'), may hold values from -6 to 6
- b_proj: bfloat16 [2048, 1024], P('ctx'), may hold values from -1.796875 to 1.796875
- c_proj: bfloat16 [2048, 1024], P('ctx'), may hold values from -1.796875 to 1.796875
- step_dt: float32 [128, 2048], P('vocab', 'ctx'), may hold values from 0.01 to 0.05
- log_decay: float32 [128, 2048], P('vocab', 'ctx'), may hold values from -2 to 0
- skip_d: float32 [128], P('vocab'), may hold values from 0.5 to 1.5
Outputs:
- grad_head: bfloat16 [4096, 32768], P('ctx', 'vocab')
- grad_resid: bfloat16 [2048, 4096], P('ctx', 'vocab')
- grad_out_weight: bfloat16 [8192, 4096], P('vocab', 'ctx')
- grad_xs: bfloat16 [2048, 8192], P('ctx', 'vocab')
- grad_gate: bfloat16 [2048, 8192], P('ctx', 'vocab')
- grad_b: bfloat16 [2048, 1024], P(('ctx', 'vocab'))
- grad_c: bfloat16 [2048, 1024], P(('ctx', 'vocab'))
- grad_dt: float32 [128, 2048], P('vocab', 'ctx')
- grad_log_decay: float32 [128, 2048], P('vocab', 'ctx')
All inputs are finite; a program needn't handle non-finite values.
Results may differ from a plain program's by a relative error of at most 0.0085.
Values may be sent and summed in bfloat16 or wider, within the bound.
A program may use at most 128 MiB of HBM per device.

v0:
```python
import jax
import jax.numpy as jnp
from jax import lax
from jax.sharding import PartitionSpec as P

D = 4096
HEAD_NUMBER = 128
HEAD_DIM = 64
GROUPS = 8
QBLK = 128
INNER = 8192


epsilon = 1e-05
precise = lax.Precision.HIGHEST


def carried_in(array, axis, combine, identity, reverse):
    length, place = (lax.axis_size(axis), lax.axis_index(axis))
    everything = jax.tree.map(lambda part: lax.all_gather(part, axis), array)
    start = jax.tree.map(
        lambda part, zero: jnp.broadcast_to(jnp.asarray(zero, part.dtype), part.shape),
        array,
        identity,
    )

    def hop(k, before):
        at = length - 1 - k if reverse else k
        reached = at > place if reverse else at < place
        new = combine(before, jax.tree.map(lambda part: part[at], everything))
        return jax.tree.map(lambda a, b: jnp.where(reached, a, b), new, before)

    return lax.fori_loop(0, length, hop, start)


def block_update(carried, segment):
    x_block, step_block, decay_block, b_block, c_block = segment
    running = jnp.cumsum(decay_block, axis=1)
    length = decay_block.shape[1]
    causal = jnp.arange(length)[:, None] >= jnp.arange(length)[None, :]
    span_decay = jnp.exp(
        jnp.where(causal[None], running[:, :, None] - running[:, None, :], -jnp.inf)
    )
    scores = (
        jnp.einsum("thn,shn->hts", c_block, b_block, precision=precise)
        * span_decay
        * step_block[:, None, :]
    )
    outputs = jnp.einsum("hts,shp->thp", scores, x_block, precision=precise)
    c_decayed = c_block * jnp.exp(running).T[:, :, None]
    outputs = outputs + jnp.einsum("thn,hnp->thp", c_decayed, carried, precision=precise)
    tail_weight = (jnp.exp(running[:, -1:] - running) * step_block).T
    update = jnp.einsum(
        "shn,shp->hnp", b_block * tail_weight[:, :, None], x_block, precision=precise
    )
    new_carried = jnp.exp(running[:, -1])[:, None, None] * carried + update
    return (new_carried, outputs)


def run_ssd(x_heads, step_rows, decay_rows, b_heads, c_heads, start_state):
    positions, head_count, channels = x_heads.shape
    blocks = positions // QBLK

    def by_rows(values):
        return values.reshape(blocks, QBLK, head_count, values.shape[2])

    def by_heads(values):
        return values.reshape(head_count, blocks, QBLK).transpose(1, 0, 2)

    final_state, outputs = lax.scan(
        block_update,
        start_state,
        (
            by_rows(x_heads),
            by_heads(step_rows),
            by_heads(decay_rows),
            by_rows(b_heads),
            by_rows(c_heads),
        ),
    )
    return (outputs.reshape(positions, head_count, channels), final_state)


def select_heads(projection, selector):
    positions = projection.shape[0]
    return jnp.einsum(
        "tgn,hg->thn", projection.reshape(positions, GROUPS, -1), selector, precision=precise
    )


def layer_core(x_float, step_rows, decay_rows, b_float, c_float, start_state, selector, skip_d):
    positions = x_float.shape[0]
    head_count = selector.shape[0]
    x_heads = x_float.reshape(positions, head_count, HEAD_DIM)
    outputs, final_state = run_ssd(
        x_heads,
        step_rows,
        decay_rows,
        select_heads(b_float, selector),
        select_heads(c_float, selector),
        start_state,
    )
    outputs = outputs + skip_d[None, :, None] * x_heads
    return (outputs.reshape(positions, head_count * HEAD_DIM), final_state)


def compose_forward(earlier, later):
    first_decay, first_summary = earlier
    second_decay, second_summary = later
    return (
        first_decay * second_decay,
        second_decay[:, None, None] * first_summary + second_summary,
    )


def compose_backward(earlier, later):
    upper_decay, upper_adjoint = earlier
    lower_decay, lower_adjoint = later
    return (lower_decay * upper_decay, lower_adjoint + lower_decay[:, None, None] * upper_adjoint)


def shards(
    resid_out,
    final_gain,
    head_weight,
    targets,
    out_weight,
    norm_gain,
    xs,
    gate_z,
    b_proj,
    c_proj,
    step_dt,
    log_decay,
    skip_d,
):
    token_count = resid_out.shape[0]
    width_local = resid_out.shape[1]
    vocab_local = head_weight.shape[1]
    heads_local = skip_d.shape[0]
    inner_local = xs.shape[1]
    vocab_index = lax.axis_index("vocab")
    stream = lax.all_gather(resid_out, "vocab", axis=1, tiled=True)
    stream_float = stream.astype(jnp.float32)
    inv_rms = lax.rsqrt(jnp.mean(stream_float * stream_float, axis=1, keepdims=True) + epsilon)
    normed = (stream_float * inv_rms * final_gain[None, :]).astype(jnp.bfloat16)
    weights = lax.all_gather(head_weight, "ctx", axis=0, tiled=True)
    logits = jnp.dot(normed, weights, preferred_element_type=jnp.float32)
    local_max = jnp.max(logits, axis=1)
    row_max = lax.pmax(local_max, "vocab")
    row_total = lax.psum(jnp.sum(jnp.exp(logits - row_max[:, None]), axis=1), "vocab")
    log_norm = row_max + jnp.log(row_total)
    vocab_ids = vocab_index * vocab_local + jnp.arange(vocab_local)
    match = (targets[:, None] == vocab_ids[None, :]).astype(jnp.float32)
    grad_logits = (jnp.exp(logits - log_norm[:, None]) - match).astype(jnp.bfloat16)
    columns = normed
    head_sum = lax.psum_scatter(
        lax.dot_general(
            columns, grad_logits, (((0,), (0,)), ((), ())), preferred_element_type=jnp.float32
        ),
        "ctx",
        scatter_dimension=0,
        tiled=True,
    )
    grad_head = head_sum.astype(jnp.bfloat16)
    stream_part = lax.dot_general(
        grad_logits, weights, (((1,), (1,)), ((), ())), preferred_element_type=jnp.float32
    )
    stream_grad = lax.psum_scatter(stream_part, "vocab", scatter_dimension=1, tiled=True)
    gain_local = lax.dynamic_slice_in_dim(final_gain, vocab_index * width_local, width_local)
    scaled = stream_grad * gain_local[None, :]
    resid_float = resid_out.astype(jnp.float32)
    inner_dot = lax.psum(jnp.sum(resid_float * scaled, axis=1), "vocab")
    grad_resid = (
        inv_rms * scaled - resid_float * inv_rms * inv_rms * inv_rms * (inner_dot / D)[:, None]
    ).astype(jnp.bfloat16)
    head_ids = vocab_index * heads_local + jnp.arange(heads_local)
    selector = (head_ids[:, None] // (HEAD_NUMBER // GROUPS) == jnp.arange(GROUPS)[None, :]).astype(
        jnp.float32
    )
    x_float = xs.astype(jnp.float32)
    b_float = b_proj.astype(jnp.float32)
    c_float = c_proj.astype(jnp.float32)
    x_heads = x_float.reshape(token_count, heads_local, HEAD_DIM)
    b_heads = select_heads(b_float, selector)
    c_heads = select_heads(c_float, selector)
    running = jnp.cumsum(log_decay, axis=1)
    shard_log = running[:, -1]
    carry_weight = jnp.exp(shard_log[:, None] - running) * step_dt
    local_state = jnp.einsum("thn,ht,thp->hnp", b_heads, carry_weight, x_heads, precision=precise)
    shard_decay = jnp.exp(shard_log)
    _, start_state = carried_in(
        (shard_decay, local_state),
        "ctx",
        compose_forward,
        (jnp.ones_like(shard_decay), jnp.zeros_like(local_state)),
        False,
    )

    def core(x_in, step_in, decay_in, b_in, c_in):
        return layer_core(x_in, step_in, decay_in, b_in, c_in, start_state, selector, skip_d)

    (ssd_out, end_state), pullback = jax.vjp(core, x_float, step_dt, log_decay, b_float, c_float)
    gate_float = gate_z.astype(jnp.float32)
    sigmoid = jax.nn.sigmoid(gate_float)
    gated = ssd_out * gate_float * sigmoid
    gated_heads = gated.reshape(token_count, heads_local, HEAD_DIM)
    group_width = INNER // GROUPS
    group_sums = lax.psum(
        jnp.dot(jnp.sum(gated_heads * gated_heads, axis=2), selector, precision=precise), "vocab"
    )
    group_inv = lax.rsqrt(group_sums / group_width + epsilon)
    head_inv = jnp.dot(group_inv, selector.T, precision=precise)
    gain_heads = norm_gain.reshape(heads_local, HEAD_DIM)
    normed_inner = (
        (gated_heads * head_inv[:, :, None] * gain_heads[None])
        .reshape(token_count, inner_local)
        .astype(jnp.bfloat16)
    )
    stream_back = lax.all_gather(grad_resid, "vocab", axis=1, tiled=True)
    out_term = lax.dot_general(
        normed_inner, stream_back, (((0,), (0,)), ((), ())), preferred_element_type=jnp.float32
    )
    grad_out_weight = lax.psum_scatter(out_term, "ctx", scatter_dimension=1, tiled=True).astype(
        jnp.bfloat16
    )
    columns = stream_back
    grad_normed = lax.dot_general(
        columns,
        lax.all_gather(out_weight, "ctx", axis=1, tiled=True),
        (((1,), (1,)), ((), ())),
        preferred_element_type=jnp.float32,
    )
    scaled_inner = grad_normed.reshape(token_count, heads_local, HEAD_DIM) * gain_heads[None]
    group_dot = lax.psum(
        jnp.dot(jnp.sum(gated_heads * scaled_inner, axis=2), selector, precision=precise), "vocab"
    )
    head_dot = jnp.dot(group_dot, selector.T, precision=precise)
    grad_gated = (
        head_inv[:, :, None] * scaled_inner
        - gated_heads * (head_inv * head_inv * head_inv * head_dot / group_width)[:, :, None]
    )
    grad_gated = grad_gated.reshape(token_count, inner_local)
    grad_gate = (grad_gated * ssd_out * sigmoid * (1.0 + gate_float * (1.0 - sigmoid))).astype(
        jnp.bfloat16
    )
    grad_ssd = grad_gated * gate_float * sigmoid
    grad_ssd_heads = grad_ssd.reshape(token_count, heads_local, HEAD_DIM)
    local_adjoint = jnp.einsum(
        "thn,ht,thp->hnp", c_heads, jnp.exp(running), grad_ssd_heads, precision=precise
    )
    _, end_adjoint = carried_in(
        (shard_decay, local_adjoint),
        "ctx",
        compose_backward,
        (jnp.ones_like(shard_decay), jnp.zeros_like(local_adjoint)),
        True,
    )
    grad_x, grad_dt, grad_decay, grad_b_float, grad_c_float = pullback((grad_ssd, end_adjoint))
    grad_b, grad_c = (
        lax.psum_scatter(grad_b_float, "vocab", scatter_dimension=0, tiled=True),
        lax.psum_scatter(grad_c_float, "vocab", scatter_dimension=0, tiled=True),
    )
    return (
        grad_head,
        grad_resid,
        grad_out_weight,
        grad_x.astype(jnp.bfloat16),
        grad_gate,
        grad_b.astype(jnp.bfloat16),
        grad_c.astype(jnp.bfloat16),
        grad_dt,
        grad_decay,
    )


def solution(mesh):
    return jax.shard_map(
        shards,
        mesh=mesh,
        in_specs=(
            P("ctx", "vocab"),
            P(),
            P("ctx", "vocab"),
            P("ctx"),
            P("vocab", "ctx"),
            P("vocab"),
            P("ctx", "vocab"),
            P("ctx", "vocab"),
            P("ctx", None),
            P("ctx", None),
            P("vocab", "ctx"),
            P("vocab", "ctx"),
            P("vocab"),
        ),
        out_specs=(
            P("ctx", "vocab"),
            P("ctx", "vocab"),
            P("vocab", "ctx"),
            P("ctx", "vocab"),
            P("ctx", "vocab"),
            P(("ctx", "vocab"), None),
            P(("ctx", "vocab"), None),
            P("vocab", "ctx"),
            P("vocab", "ctx"),
        ),
        check_vma=False,
    )
```

profile of v0, /device:TPU:1, one launch (start us, length us, event | category | flops | bytes accessed | tf_op | source)
XLA Modules:
  0.0 1463.4 jit_solution(10675571212429738081)
XLA Ops:
  10.6 1.2 reduce-window.6
  15.7 69.4 %all-gather.10.cloned.1.call-done = bf16[256,4096]{1,0:T(8,128)(2,1)} async-done(((bf16[256,128]{1,0:T(8,128)(2,1)}), bf16[256,4096]{1,0:T(8,128)(2,1)}) %all-gather.10.cloned.1.call-update) | async-done | bytes 2097168 | tf_op jit(solution)/shard_map/all_gather | solution.py:143
  85.2 2.1 fusion.83
  87.3 55.3 %all-gather.12.cloned.1.call-done = bf16[4096,1024]{1,0:T(8,128)(2,1)} async-done(((bf16[512,1024]{1,0:T(8,128)(2,1)}), bf16[4096,1024]{1,0:T(8,128)(2,1)}) %all-gather.12.cloned.1.call-update) | async-done | bytes 8388624 | tf_op jit(solution)/shard_map/all_gather | solution.py:147
  142.6 6.5 fusion.146
  149.1 61.2 %pmax.7 = f32[256]{0:T(256)S(1)} all-reduce(f32[256]{0:T(256)S(1)} %get-tuple-element.1550), channel_id=1, replica_groups=mesh['ctx'=8,'vocab'=32] {'vocab'}, use_global_device_ids=true, to_apply=%region_2.0 | all-reduce | flops 256 | bytes 2048 | tf_op jit(solution)/shard_map/pmax | solution.py:150
  210.5 55.7 %psum.28 = f32[256]{0:T(256)S(1)} all-reduce(f32[256]{0:T(256)S(1)} %exponential_reduce_fusion.1), channel_id=1, replica_groups=mesh['ctx'=8,'vocab'=32] {'vocab'}, use_global_device_ids=true, to_apply=%region_4.0 | all-reduce | flops 256 | bytes 2048 | tf_op jit(solution)/shard_map/psum | solution.py:151
  266.3 7.8 fusion.142
  276.6 40.1 %all-reduce.2 = f32[32]{0:T(128)S(1)} all-reduce(f32[32]{0:T(128)S(1)} %dynamic-update-slice), channel_id=2, replica_groups=mesh['ctx'=8,'vocab'=32] {'ctx'}, use_global_device_ids=true, to_apply=%add.2 | all-reduce | flops 32 | bytes 256
  318.4 9.6 while.100
  328.2 187.2 %reduce-scatter.8.cloned.1.call-done = f32[256,128]{1,0:T(8,128)} async-done(((f32[256,4096]{1,0:T(8,128)}), f32[256,128]{1,0:T(8,128)}) %reduce-scatter.8.cloned.1.call-update) | async-done | bytes 131088 | tf_op jit(solution)/shard_map/reduce_scatter | solution.py:169
  516.4 58.6 %psum.29 = f32[256]{0:T(256)S(1)} all-reduce(f32[256]{0:T(256)S(1)} %fusion.118), channel_id=1, replica_groups=mesh['ctx'=8,'vocab'=32] {'vocab'}, use_global_device_ids=true, to_apply=%region_8.0 | all-reduce | flops 256 | bytes 2048 | tf_op jit(solution)/shard_map/psum | solution.py:173
  575.0 1.7 fusion.117
  577.1 17.8 %while.99 = (s32[]{:T(128)}, f32[4,128,64]{1,2,0:T(8,128)S(1)}, f32[2,128,4,64]{1,0,3,2:T(2,128)S(1)}, f32[2,4,128,128]{3,2,1,0:T(8,128)S(1)}, f32[2,4,128,128]{...) while((s32[]{:T(128)}, f32[4,128,64]{1,2,0:T(8,128)S(1)}, ...), condition=%wide.region_15.16_spmd.clone.clone, body=%wide.region_13.15_spmd.clone.clone.sunk | while | flops 252741632 | bytes 6406041 | solution.py:70
  578.7 1.6 bitcast_dynamic-update-slice_fusion.6
  581.7 2.6 dynamic_update_slice.203
  587.6 1.6 bitcast_dynamic-update-slice_fusion.6
  590.6 2.6 dynamic_update_slice.203
  594.9 64.9 %all-gather.14.cloned.1.call-done = bf16[256,4096]{1,0:T(8,128)(2,1)} async-done(((bf16[256,128]{1,0:T(8,128)(2,1)}), bf16[256,4096]{1,0:T(8,128)(2,1)}) %all-gather.14.cloned.1.call-update) | async-done | bytes 2097168 | tf_op jit(solution)/shard_map/all_gather | solution.py:220
  659.8 3.0 multiply_reduce_fusion
  663.3 114.3 %all-reduce.3 = (f32[256,8]{0,1:T(8,128)S(1)}, f32[256,8]{0,1:T(8,128)S(1)}) all-reduce(f32[256,8]{0,1:T(8,128)S(1)} %fusion.128, f32[256,8]{0,1:T(8,128)S(1)} %fusion.127), channel_id=1, replica_groups=mesh['ctx'=8,'vocab'=32] {'vocab'}, use_global_device_ids=true, to_apply=%region_17.18 | all-reduce | flops 4096 | bytes 32768 | tf_op jit(solution)/shard_map/psum | solution.py:209
  778.9 2.2 fusion.95
  782.1 50.9 %all-gather.20.cloned.1.call-done = f32[32,128,64]{1,2,0:T(8,128)} async-done(((f32[4,128,64]{1,2,0:T(8,128)}), f32[32,128,64]{1,2,0:T(8,128)}) %all-gather.20.cloned.1.call-update) | async-done | bytes 1048592 | tf_op jit(solution)/shard_map/all_gather | solution.py:20
  833.0 9.7 while.101
  845.2 33.2 %while.98 = (s32[]{:T(128)}, f32[4,128,64]{1,2,0:T(8,128)S(1)}, f32[2,128,4,64]{1,0,3,2:T(2,128)}, f32[2,4,128]{2,1,0:T(4,128)S(1)}, f32[2,4,128]{2,1,0:T(4,128)...) while((s32[]{:T(128)}, f32[4,128,64]{1,2,0:T(8,128)S(1)}, ...), condition=%wide.region_32.33_spmd.clone, body=%wide.region_23.32_spmd.clone.sunk | while | flops 504861184 | bytes 15032001 | solution.py:70
  846.4 1.7 fusion.214
  853.6 1.3 reduce_window_sum.54
  854.9 1.6 convolution_bitcast_fusion.10
  856.4 1.3 fusion.212
  857.8 2.6 dynamic_update_slice.195
  860.4 1.4 convolution_add_fusion.4
  862.9 1.7 fusion.214
  870.2 1.3 reduce_window_sum.54
  871.4 1.6 convolution_bitcast_fusion.10
  873.0 1.3 fusion.212
  874.3 2.6 dynamic_update_slice.195
  877.0 1.4 convolution_add_fusion.4
  878.4 2.1 fusion.93
  884.1 4.4 fusion.147
  888.7 8.3 fusion.87
  899.6 193.5 %reduce-scatter.12.cloned.1.call-done = f32[8,1024]{1,0:T(8,128)} async-done(((f32[256,1024]{1,0:T(8,128)}), f32[8,1024]{1,0:T(8,128)}) %reduce-scatter.12.cloned.1.call-update) | async-done | bytes 32784 | tf_op jit(solution)/shard_map/reduce_scatter | solution.py:261
  1093.2 1.4 convert_element_type.61
  1094.5 217.7 %reduce-scatter.14.cloned.1.call-done = f32[8,1024]{1,0:T(8,128)} async-done(((f32[256,1024]{1,0:T(8,128)}), f32[8,1024]{1,0:T(8,128)}) %reduce-scatter.14.cloned.1.call-update) | async-done | bytes 32784 | tf_op jit(solution)/shard_map/reduce_scatter | solution.py:262
  1312.2 1.4 convert_element_type.62
  1313.6 42.4 %reduce-scatter.10.cloned.1.call-done = f32[256,512]{1,0:T(8,128)} async-done(((f32[256,4096]{1,0:T(8,128)}), f32[256,512]{1,0:T(8,128)}) %reduce-scatter.10.cloned.1.call-update) | async-done | bytes 524304 | tf_op jit(solution)/shard_map/reduce_scatter | solution.py:224
  1356.0 1.8 convert_element_type.58
  1357.8 96.4 %reduce-scatter.6.cloned.1.call-done = f32[512,1024]{1,0:T(8,128)} async-done(((f32[4096,1024]{1,0:T(8,128)}), f32[512,1024]{1,0:T(8,128)}) %reduce-scatter.6.cloned.1.call-update) | async-done | bytes 2097168 | tf_op jit(solution)/shard_map/reduce_scatter | solution.py:157
  1454.2 2.7 convert_element_type.52
  (296 shorter events, 65.0 us)
Async XLA Ops:
  7.2 135.4 %copy-start.15 = (f32[4096]{0:T(1024)S(1)}, f32[4096]{0:T(1024)}, u32[]{:S(2)}) copy-start(f32[4096]{0:T(1024)} %param.22) | copy-start | bytes 49156
  7.2 78.0 %all-gather.10.cloned.1.call-start = ((), (), s32[]{:S(2)}) async-start(), calls=%async_computation.5 | async-start | bytes 2162688 | tf_op jit(solution)/shard_map/all_gather | solution.py:143
  7.9 134.6 %all-gather.12.cloned.1.call-start = ((), (), s32[]{:S(2)}) async-start(), calls=%async_computation.6 | async-start | bytes 9437184 | tf_op jit(solution)/shard_map/all_gather | solution.py:147
  8.7 309.8 %all-gather.18.cloned.1.call-start = ((), (), s32[]{:S(2)}) async-start(), calls=%async_computation.14 | async-start | bytes 1179648 | tf_op jit(solution)/shard_map/all_gather | solution.py:20
  15.7 499.7 %reduce-scatter.8.cloned.1.call-start = ((), (), s32[]{:S(2)}) async-start(), calls=%async_computation.8 | async-start | bytes 4325376 | tf_op jit(solution)/shard_map/reduce_scatter | solution.py:169
  87.3 179.0 %copy-start.20 = (s32[256]{0:T(256)S(1)}, s32[256]{0:T(256)}, u32[]{:S(2)}) copy-start(s32[256]{0:T(256)} %param.24) | copy-start | bytes 3076
  149.0 125.0 %copy-start.1 = (f32[256,1024]{1,0:T(8,128)}, f32[256,1024]{1,0:T(8,128)S(1)}, u32[]{:S(2)}) copy-start(f32[256,1024]{1,0:T(8,128)S(1)} %get-tuple-element.1551) | copy-start | bytes 3145732
  274.1 1.1 copy-start.22
  274.1 42.7 %copy-start.12 = (bf16[256,1024]{1,0:T(8,128)(2,1)S(1)}, bf16[256,1024]{1,0:T(8,128)(2,1)}, u32[]{:S(2)}) copy-start(bf16[256,1024]{1,0:T(8,128)(2,1)} %param.30) | copy-start | bytes 1572868
  274.1 44.0 %copy-start.21 = (f32[4]{0:T(128)S(1)}, f32[4]{0:T(128)}, u32[]{:S(2)}) copy-start(f32[4]{0:T(128)} %param.33) | copy-start | bytes 52
  274.1 44.1 %copy-start.14 = (bf16[256,256]{1,0:T(8,128)(2,1)S(1)}, bf16[256,256]{1,0:T(8,128)(2,1)}, u32[]{:S(2)}) copy-start(bf16[256,256]{1,0:T(8,128)(2,1)} %param.28) | copy-start | bytes 393220
  274.1 44.2 %copy-start.17 = (f32[256]{0:T(256)S(1)}, f32[256]{0:T(256)}, u32[]{:S(2)}) copy-start(f32[256]{0:T(256)} %param.26) | copy-start | bytes 3076
  274.1 320.7 %all-gather.16.cloned.1.call-start = ((), (), s32[]{:S(2)}) async-start(), calls=%async_computation.11 | async-start | bytes 2359296 | tf_op jit(solution)/shard_map/all_gather | solution.py:230
  274.7 385.1 %all-gather.14.cloned.1.call-start = ((), (), s32[]{:S(2)}) async-start(), calls=%async_computation.9 | async-start | bytes 2162688 | tf_op jit(solution)/shard_map/all_gather | solution.py:220
  318.0 197.3 %copy-start.9 = (bf16[256,128]{1,0:T(8,128)(2,1)S(1)}, bf16[256,128]{1,0:T(8,128)(2,1)}, u32[]{:S(2)}) copy-start(bf16[256,128]{1,0:T(8,128)(2,1)} %param.21) | copy-start | bytes 196612
  318.4 258.6 %copy-start.13 = (f32[4,256]{1,0:T(4,128)S(1)}, f32[4,256]{1,0:T(4,128)}, u32[]{:S(2)}) copy-start(f32[4,256]{1,0:T(4,128)} %param.31) | copy-start | bytes 12292
  318.4 258.6 %copy-start.16 = (f32[4,256]{1,0:T(4,128)S(1)}, f32[4,256]{1,0:T(4,128)}, u32[]{:S(2)}) copy-start(f32[4,256]{1,0:T(4,128)} %param.32) | copy-start | bytes 12292
  576.7 256.3 %all-gather.20.cloned.1.call-start = ((), (), s32[]{:S(2)}) async-start(), calls=%async_computation.15 | async-start | bytes 1179648 | tf_op jit(solution)/shard_map/all_gather | solution.py:20
  778.9 54.1 %copy-start.3 = (f32[256,256]{0,1:T(8,128)}, f32[256,256]{0,1:T(8,128)S(1)}, u32[]{:S(2)}) copy-start(f32[256,256]{0,1:T(8,128)S(1)} %get-tuple-element.1546) | copy-start | bytes 786436
  781.2 312.0 %reduce-scatter.12.cloned.1.call-start = ((), (), s32[]{:S(2)}) async-start(), calls=%async_computation.12 | async-start | bytes 1081344 | tf_op jit(solution)/shard_map/reduce_scatter | solution.py:261
  850.7 7.0 copy-start.6
  860.4 1.4 copy-start.7
  867.3 7.0 copy-start.6
  877.0 1.4 copy-start.7
  878.4 5.5 copy-start.18
  878.4 5.5 copy-start.19
  878.4 3.4 copy-start.5
  880.5 3.5 copy-start.10
  881.7 430.5 %reduce-scatter.14.cloned.1.call-start = ((), (), s32[]{:S(2)}) async-start(), calls=%async_computation.13 | async-start | bytes 1081344 | tf_op jit(solution)/shard_map/reduce_scatter | solution.py:262
  884.0 472.0 %reduce-scatter.10.cloned.1.call-start = ((), (), s32[]{:S(2)}) async-start(), calls=%async_computation.10 | async-start | bytes 4718592 | tf_op jit(solution)/shard_map/reduce_scatter | solution.py:224
  884.0 4.7 copy-start
  884.0 4.7 copy-start.2
  888.5 565.7 %reduce-scatter.6.cloned.1.call-start = ((), (), s32[]{:S(2)}) async-start(), calls=%async_computation.7 | async-start | bytes 18874368 | tf_op jit(solution)/shard_map/reduce_scatter | solution.py:157
  897.1 0.9 copy-start.11
  897.1 1.7 copy-start.4
  897.1 1.7 copy-start.8
Sparse Core Ops, SparseCore 0:
  10.5 74.6 all-gather.9
  87.0 55.4 all-gather.11
  145.0 25.9 all-gather.17
  274.3 241.0 reduce-scatter.7
  517.0 31.2 all-gather.15
  576.8 82.9 all-gather.13
  781.3 51.6 all-gather.19
  881.9 211.2 reduce-scatter.11
  1097.0 215.1 reduce-scatter.13
  1314.6 41.3 reduce-scatter.9
  1358.6 95.4 reduce-scatter.5
where the time goes:
time: 1460 us
  waiting for transfers between devices  980 us (67%)
  blocking collectives  330 us (23%)
  matrix products  62 us (4%)
  local copies, waits for them, and re-layouts  50.9 us (3%)
  other arithmetic  23.7 us (2%)
  between operations  15.1 us (1%)
    reduce_scatter x1, waiting for transfers between devices, shards(): lax.psum_scatter(grad_c_float, 'vocab', scatter_dimension=0, tiled=True)  218 us
    reduce_scatter x1, waiting for transfers between devices, shards(): lax.psum_scatter(grad_b_float, 'vocab', scatter_dimension=0, tiled=True)  194 us
    reduce_scatter x1, waiting for transfers between devices, shards(): lax.psum_scatter(stream_part, 'vocab', scatter_dimension=1, tiled=True)  187 us
    psum x1, blocking collectives, shards(): lax.psum(jnp.dot(jnp.sum(gated_heads * gated_heads, axis=2), selector, pr...  114 us
    reduce_scatter x1, waiting for transfers between devices, shards(): lax.psum_scatter(lax.dot_general(columns, grad_logits, (((0,), (0,)), (()...  96.4 us
    all_gather x1, waiting for transfers between devices, shards(): stream = lax.all_gather(resid_out, 'vocab', axis=1, tiled=True)  69.4 us
    all_gather x1, waiting for transfers between devices, shards(): stream_back = lax.all_gather(grad_resid, 'vocab', axis=1, tiled=True)  64.9 us
    pmax x1, blocking collectives, shards(): row_max = lax.pmax(local_max, 'vocab')  61.2 us
  transfers between devices with their start and end apart: 11, of which 9 were waited for; matrix products, arithmetic and copies ran while one was open for 5% of the time, Pallas kernels for 0%

commit v1 on v0

v1 whole, which is shorter than its diff:
```python
import functools

import jax
import jax.numpy as jnp
from jax import lax
from jax.experimental import pallas as pl
from jax.experimental.pallas import tpu as pltpu
from jax.sharding import PartitionSpec as P

MESH = pl.DeviceIdType.MESH
F32 = jnp.float32
BF16 = jnp.bfloat16
D = 4096
INNER = 8192
GROUPS = 8
EPS = 1e-05
CTX = 8
VOC = 32
TOK = 256
HIGH = lax.Precision.HIGHEST
STATE_ROWS = 160
HALF = TOK // 2


def dot(a, b, ca=1, cb=0):
    return lax.dot_general(a, b, (((ca,), (cb,)), ((), ())), preferred_element_type=F32)


def dot_high(a, b, ca=1, cb=0):
    return lax.dot_general(
        a, b, (((ca,), (cb,)), ((), ())), precision=HIGH, preferred_element_type=F32
    )


def halves(a):
    high = a.astype(BF16)
    return high, (a - high.astype(F32)).astype(BF16)


def dot_left(a, b, ca=1, cb=0):
    high, low = halves(a)
    return dot(high, b, ca, cb) + dot(low, b, ca, cb)


def dot_right(a, b, ca=1, cb=0):
    high, low = halves(b)
    return dot(a, high, ca, cb) + dot(a, low, ca, cb)


def dot_both(a, b, ca=1, cb=0):
    ah, al = halves(a)
    bh, bl = halves(b)
    return dot(ah, bh, ca, cb) + (dot(al, bh, ca, cb) + dot(ah, bl, ca, cb))


def column(row):
    return jnp.broadcast_to(row, (128, row.shape[1])).T


def row_of(col):
    return col.T[0:1]


def wide(col, lanes):
    return jnp.concatenate([col] * (lanes // 128), axis=1)


def send(src, dst, ssem, rsem, device):
    copy = pltpu.make_async_remote_copy(
        src_ref=src, dst_ref=dst, send_sem=ssem, recv_sem=rsem, device_id=device, device_id_type=MESH
    )
    copy.start()


class Ctx:
    def __init__(self, buf, ssem, rsem, c):
        y, k = c // 2, c % 2
        self.buf, self.s, self.r, self.c = buf, ssem, rsem, c
        at = lambda dy, kk: ((y + dy) % 4) * 2 + kk
        self.own, self.yp, self.ym, self.y2 = c, at(1, k), at(3, k), at(2, k)
        self.sib, self.syp, self.sym, self.sy2 = at(0, 1 - k), at(1, 1 - k), at(3, 1 - k), at(2, 1 - k)
        rows = buf.shape[1]
        self.top, self.bottom = pl.ds(0, rows // 2), pl.ds(rows // 2, rows // 2)

    def ref(self, block, part=None):
        return self.buf.at[block] if part is None else self.buf.at[block, part]

    def go(self, slot, block, to, part=None):
        ref = self.ref(block, part)
        send(ref, ref, self.s.at[slot], self.r.at[slot], {"ctx": to})

    def got(self, slot, block, part=None):
        ref = self.ref(block, part)
        pltpu.make_async_remote_copy(
            src_ref=ref, dst_ref=ref, send_sem=self.s.at[slot], recv_sem=self.r.at[slot],
            device_id={"ctx": self.sib}, device_id_type=MESH,
        ).wait_recv()

    def sent(self, slot, block, part=None):
        ref = self.ref(block, part)
        pltpu.make_async_remote_copy(
            src_ref=ref, dst_ref=ref, send_sem=self.s.at[slot], recv_sem=self.r.at[slot],
            device_id={"ctx": self.sib}, device_id_type=MESH,
        ).wait_send()

    def start(self):
        self.go(0, self.own, self.yp)
        self.go(1, self.own, self.ym)
        self.go(2, self.own, self.sib)

    def middle(self):
        self.got(0, self.ym)
        self.go(5, self.ym, self.yp, self.top)
        self.go(3, self.ym, self.sib)
        self.got(1, self.yp)
        self.go(6, self.yp, self.ym, self.bottom)
        self.go(4, self.yp, self.sib)

    def end(self):
        self.got(5, self.y2, self.top)
        self.go(7, self.y2, self.sib, self.top)
        self.got(6, self.y2, self.bottom)
        self.go(8, self.y2, self.sib, self.bottom)

    def finish(self):
        self.got(2, self.sib)
        self.got(3, self.sym)
        self.got(4, self.syp)
        self.last()

    def last(self):
        self.got(7, self.sy2, self.top)
        self.got(8, self.sy2, self.bottom)

    def drain(self):
        self.sent(0, self.own)
        self.sent(1, self.own)
        self.sent(2, self.own)
        self.sent(3, self.ym)
        self.sent(4, self.yp)
        self.sent(5, self.ym, self.top)
        self.sent(6, self.yp, self.bottom)
        self.sent(7, self.y2, self.top)
        self.sent(8, self.y2, self.bottom)


ORDER = (0, 1, 7, 2, 6, 3, 5, 4)


class Voc:
    def __init__(self, buf, ssem, rsem, v):
        self.buf, self.s, self.r = buf, ssem, rsem
        self.x, self.z = v // 8, v % 8
        self.v = v
        self.xp, self.xm = (self.x + 1) % 4, (self.x + 3) % 4

    def wait(self, refs, sem_s, sem_r, receive):
        copy = pltpu.make_async_remote_copy(
            src_ref=refs, dst_ref=refs, send_sem=sem_s, recv_sem=sem_r,
            device_id={"vocab": self.xp * 8 + self.z}, device_id_type=MESH,
        )
        if receive:
            copy.wait_recv()
        else:
            copy.wait_send()

    def start(self):
        for d in ORDER[1:]:
            ref = self.buf.at[self.v]
            send(ref, ref, self.s.at[0], self.r.at[d], {"vocab": self.x * 8 + (self.z + d) % 8})

    def spread(self):
        for d in ORDER:
            ref = self.buf.at[self.x * 8 + (self.z + 8 - d) % 8]
            if d:
                self.wait(ref, self.s.at[0], self.r.at[d], True)
            send(ref, ref, self.s.at[1], self.r.at[8 + d], {"vocab": self.xp * 8 + self.z})
            send(ref, ref, self.s.at[2], self.r.at[16 + d], {"vocab": self.xm * 8 + self.z})

    def relay(self):
        for d in ORDER:
            zz = (self.z + 8 - d) % 8
            block = self.xm * 8 + zz
            self.wait(self.buf.at[block], self.s.at[1], self.r.at[8 + d], True)
            ref = self.buf.at[block, pl.ds(0, HALF)]
            send(ref, ref, self.s.at[3], self.r.at[24 + d], {"vocab": self.xp * 8 + self.z})
            block = self.xp * 8 + zz
            self.wait(self.buf.at[block], self.s.at[2], self.r.at[16 + d], True)
            ref = self.buf.at[block, pl.ds(HALF, HALF)]
            send(ref, ref, self.s.at[4], self.r.at[32 + d], {"vocab": self.xm * 8 + self.z})

    def finish(self):
        for d in ORDER:
            block = ((self.x + 2) % 4) * 8 + (self.z + 8 - d) % 8
            self.wait(self.buf.at[block, pl.ds(0, HALF)], self.s.at[3], self.r.at[24 + d], True)
            self.wait(self.buf.at[block, pl.ds(HALF, HALF)], self.s.at[4], self.r.at[32 + d], True)

    def drain(self):
        self.wait(self.buf.at[pl.ds(0, 7)], self.s.at[0], self.r.at[0], False)
        self.wait(self.buf.at[pl.ds(0, 8)], self.s.at[1], self.r.at[0], False)
        self.wait(self.buf.at[pl.ds(0, 8)], self.s.at[2], self.r.at[0], False)
        self.wait(self.buf.at[pl.ds(0, 4)], self.s.at[3], self.r.at[0], False)
        self.wait(self.buf.at[pl.ds(0, 4)], self.s.at[4], self.r.at[0], False)


class Many:
    def __init__(self, axis, me, peer, count, src, dst, ssem, rsem):
        self.axis, self.me, self.peer, self.count = axis, me, peer, count
        self.src, self.dst, self.ssem, self.rsem = src, dst, ssem, rsem

    def start(self, slot):
        @pl.loop(1, self.count)
        def _(d):
            to = self.peer(d)
            send(self.src(to), self.dst.at[slot], self.ssem, self.rsem, {self.axis: to})

    def whole(self):
        refs = self.dst.at[pl.ds(0, self.count - 1)]
        return pltpu.make_async_remote_copy(
            src_ref=refs, dst_ref=refs, send_sem=self.ssem, recv_sem=self.rsem,
            device_id={self.axis: self.peer(1)}, device_id_type=MESH,
        )

    def got(self):
        self.whole().wait_recv()

    def drain(self):
        self.whole().wait_send()


def kernel(*refs):
    (resid, gain, head_w, target, out_w, norm_gain, xs, gate, b_in, c_in, dt_in, decay_in, skip_in) = refs[:13]
    (gh_o, gr_o, gow_o, gx_o, gg_o, gb_o, gc_o, gdt_o, gld_o) = refs[13:22]
    (wbuf, owbuf, sbuf, nbuf, ntsend, ntbuf, logits, gall, pbuf, rel_a, rel_b, from_m, from_p, rz, gbuf,
     ubuf, vbuf, osend, obuf, es, acc, lse_b, inner_b, gsum_b, gdot_b, mean_s, mean_b, bcs, bcr, mcol, ycur, cbb, cb_ch0, gyb,
     lsem, ws, wr, ows, owr, gs, gr, us, ur, vs, vr, s1s, s1r, s2s, s2r, rs_s, rs_r, ms, mr) = refs[22:]
    c = lax.axis_index("ctx")
    v = lax.axis_index("vocab")
    x, z = v // 8, v % 8
    xp, xm, x2 = (x + 1) % 4, (x + 3) % 4, (x + 2) % 4

    barrier = pltpu.get_barrier_semaphore()

    @pl.loop(1, VOC)
    def _(d):
        pl.semaphore_signal(barrier, inc=1, device_id={"vocab": (v + d) % VOC}, device_id_type=MESH)

    @pl.loop(1, CTX)
    def _(d):
        pl.semaphore_signal(barrier, inc=1, device_id={"ctx": (c + d) % CTX}, device_id_type=MESH)

    local = [
        pltpu.make_async_copy(resid, sbuf.at[v], lsem.at[0]),
        pltpu.make_async_copy(head_w, wbuf.at[c], lsem.at[1]),
        pltpu.make_async_copy(out_w, owbuf.at[c], lsem.at[2]),
    ]
    for copy in local:
        copy.start()
    for copy in local:
        copy.wait()
    pl.semaphore_wait(barrier, VOC + CTX - 2)

    weights = Ctx(wbuf, ws, wr, c)
    outs_w = Ctx(owbuf, ows, owr, c)
    grads = Ctx(gall, gs, gr, c)
    states = Ctx(ubuf, us, ur, c)
    adjoints = Ctx(vbuf, vs, vr, c)
    stream = Voc(sbuf, s1s, s1r, v)
    back = Voc(gbuf, s2s, s2r, v)
    over_v = lambda d: (v + d) % VOC
    over_c = lambda d: (c + d) % CTX
    quarter = (v // 4) * 4
    over_g = lambda d: quarter + (v % 4 + d) % 4
    lse_x = Many("vocab", v, over_v, VOC, lambda to: lse_b.at[v], lse_b, ms.at[0], mr.at[0])
    inner_x = Many("vocab", v, over_v, VOC, lambda to: inner_b.at[v], inner_b, ms.at[1], mr.at[1])
    gsum_x = Many("vocab", v, over_g, 4, lambda to: gsum_b.at[v % 4], gsum_b, ms.at[2], mr.at[2])
    gdot_x = Many("vocab", v, over_g, 4, lambda to: gdot_b.at[v % 4], gdot_b, ms.at[3], mr.at[3])
    norm_x = Many("ctx", c, over_c, CTX, lambda to: ntsend.at[to], ntbuf, ms.at[4], mr.at[4])
    out_x = Many("ctx", c, over_c, CTX, lambda to: osend.at[to], obuf, ms.at[5], mr.at[5])
    bc_x = Many("vocab", v, over_v, VOC, lambda to: bcs.at[to], bcr, ms.at[6], mr.at[6])
    mean_x = Many("vocab", v, over_v, VOC, lambda to: mean_s.at[to], mean_b, ms.at[7], mr.at[7])

    stream.start()
    weights.start()
    stream.spread()

    group = v // 4
    lanes = pl.ds(pl.multiple_of(group * 128, 128), 128)
    b = b_in[:, lanes]
    cc = c_in[:, lanes]
    xb = xs[...]
    xf = xb.astype(F32)
    row_i = lax.broadcasted_iota(jnp.int32, (TOK, TOK), 0)
    col_i = lax.broadcasted_iota(jnp.int32, (TOK, TOK), 1)
    upper = (row_i <= col_i).astype(F32)
    head_of = lax.broadcasted_iota(jnp.int32, (8, TOK), 1) // 64
    sel = (head_of == lax.broadcasted_iota(jnp.int32, (8, TOK), 0)).astype(F32)
    dt = dt_in[...]
    a = dot_high(decay_in[...], upper)
    last = a[:, TOK - 1 :]
    tail = jnp.exp(last - a) * dt
    a_cols = jnp.concatenate([a] * 16, axis=0).T
    cbb[...] = dot(cc, b, 1, 1)
    low = lax.broadcasted_iota(jnp.int32, (TOK, 128), 1) < 64
    for pair in range(2):
        outs = []
        for h in (2 * pair, 2 * pair + 1):
            gap = a_cols[:, h : h + 1] - a[h : h + 1]
            e = jnp.exp(jnp.where(row_i >= col_i, gap, -1e30)) * dt[h : h + 1]
            es[h] = e
            outs.append(dot_left(cbb[...] * e, xb[:, pair * 128 : pair * 128 + 128]))
        ycur[:, pair * 128 : pair * 128 + 128] = jnp.where(low, outs[0], outs[1])
    tail_full = dot_high(tail, sel, 0, 0)
    grow_full = dot_high(jnp.exp(a), sel, 0, 0)
    ubuf[c, 0:128] = dot_right(b, tail_full * xf, 0, 0)
    whole = dot_high(jnp.broadcast_to(jnp.exp(last), (8, 128)), sel, 0, 0)
    ubuf[c, 128:STATE_ROWS] = whole[0 : STATE_ROWS - 128]

    stream.relay()
    weights.middle()
    stream.finish()

    def square(i, total):
        block = sbuf[i].astype(F32)
        return total + block * block

    total = lax.fori_loop(0, VOC, square, jnp.zeros((TOK, 128), F32))
    inv = lax.rsqrt(jnp.sum(total, axis=1, keepdims=True) * (1.0 / D) + EPS)
    inv = jnp.broadcast_to(inv, (TOK, 128))

    @pl.loop(0, CTX)
    def _(i):
        parts = []
        for j in range(4):
            parts.append((sbuf[4 * i + j].astype(F32) * inv * gain[4 * i + j]).astype(BF16))
        block = jnp.concatenate(parts, axis=1)
        nbuf[i] = block
        ntsend[i] = block.T

    ntbuf[c] = ntsend[c]

    def logit(i, first=False):
        part = dot(nbuf[i], wbuf[i])
        if first:
            logits[...] = part
        else:
            logits[...] += part

    logit(weights.own, True)
    weights.got(2, weights.sib)
    logit(weights.sib)
    logit(weights.ym)
    logit(weights.yp)
    weights.end()
    logit(weights.y2)
    weights.got(3, weights.sym)
    logit(weights.sym)
    weights.got(4, weights.syp)
    logit(weights.syp)
    weights.last()
    logit(weights.sy2)

    states.start()
    outs_w.start()
    norm_x.start(c)

    @pl.loop(0, 4)
    def _(i):
        rows = pl.ds(pl.multiple_of(i * 64, 64), 64)
        part = logits[rows, :]
        most = jnp.max(part, axis=1, keepdims=True)
        value = most + jnp.log(jnp.sum(jnp.exp(part - most), axis=1, keepdims=True))
        mcol[rows, :] = jnp.broadcast_to(value, (64, 128))

    lse_b[v] = row_of(mcol[...])
    lse_x.start(v)
    target_col = column(target[...])
    states.middle()
    lse_x.got()
    every = lse_b[...]
    most = jnp.max(every, axis=0)
    log_norm = most + jnp.log(jnp.sum(jnp.exp(every - most[None]), axis=0))
    mcol[...] = column(log_norm)
    cb_ch0[:, 0:128] = target_col

    base = (v * 1024).astype(F32)
    ids = lax.broadcasted_iota(jnp.int32, (64, 1024), 1).astype(F32) + base

    @pl.loop(0, 4)
    def _(i):
        rows = pl.ds(pl.multiple_of(i * 64, 64), 64)
        part = logits[rows, :]
        hit = jnp.where(wide(cb_ch0[rows, 0:128], 1024) == ids, 1.0, 0.0)
        g = (jnp.exp(part - wide(mcol[rows, :], 1024)) - hit).astype(BF16)
        gall[c, rows, :] = g
        value = jnp.sum(g.astype(F32) * part, axis=1, keepdims=True)
        mcol[rows, :] = jnp.broadcast_to(value, (64, 128))
        value = jnp.sum(g.astype(F32), axis=1, keepdims=True)
        cb_ch0[rows, 128:256] = jnp.broadcast_to(value, (64, 128))

    inner_b[v, 0:1] = row_of(mcol[...])
    inner_b[v, 1:2] = row_of(cb_ch0[:, 128:256])
    inner_x.start(v)

    weigh = jnp.concatenate([gall[c], jnp.full((16, 1024), 2.0**-10, BF16)], axis=0)
    sums_g = cb_ch0[:, 128:256]

    def partial(i):
        part = dot(weigh, wbuf[i], 1, 1)
        for j in range(4):
            mean = part[TOK : TOK + 1, j * 128 : j * 128 + 128]
            mean_s[4 * i + j] = mean
            pbuf[4 * i + j] = (part[0:TOK, j * 128 : j * 128 + 128] - sums_g * mean).astype(BF16)

    rs = lambda i: (rs_s.at[i], rs_r.at[i])
    to_p, to_m = {"vocab": xp * 8 + z}, {"vocab": xm * 8 + z}

    def rs_wait(ref, i, receive=True):
        copy = pltpu.make_async_remote_copy(
            src_ref=ref, dst_ref=ref, send_sem=rs_s.at[i], recv_sem=rs_r.at[i], device_id=to_p, device_id_type=MESH
        )
        if receive:
            copy.wait_recv()
        else:
            copy.wait_send()

    top, bottom = pl.ds(0, HALF), pl.ds(HALF, HALF)
    far, near = 1 - z // 4, z // 4
    for n, h in enumerate((far, near)):
        partial(2 * x2 + h)
        four = pl.ds(4 * (2 * x2 + h), 4)
        send(pbuf.at[four, top], rel_a.at[n], *rs(n), to_p)
        send(pbuf.at[four, bottom], rel_b.at[n], *rs(2 + n), to_m)
    grads.start()
    for n, h in enumerate((far, near)):
        partial(2 * xp + h)
        partial(2 * xm + h)
    for n, h in enumerate((far, near)):
        partial(2 * x + h)
    mean_b[v] = mean_s[v]
    mean_x.start(v)
    states.end()
    outs_w.middle()
    for n, h in enumerate((far, near)):
        rs_wait(rel_a.at[n], n)
        for j in range(4):
            i = 4 * (2 * xp + h) + j
            pbuf[i, 0:HALF] = (pbuf[i, 0:HALF].astype(F32) + rel_a[n, j].astype(F32)).astype(BF16)
        send(pbuf.at[pl.ds(4 * (2 * xp + h), 4)], from_m.at[n], *rs(4 + n), to_p)
        rs_wait(rel_b.at[n], 2 + n)
        for j in range(4):
            i = 4 * (2 * xm + h) + j
            pbuf[i, HALF:TOK] = (pbuf[i, HALF:TOK].astype(F32) + rel_b[n, j].astype(F32)).astype(BF16)
        send(pbuf.at[pl.ds(4 * (2 * xm + h), 4)], from_p.at[n], *rs(6 + n), to_m)

    states.finish()

    def enter(j, h0):
        new = ubuf[j, 128:129] * h0 + ubuf[j, 0:128]
        return jnp.where(j < c, new, h0)

    h0 = lax.fori_loop(0, CTX - 1, enter, jnp.zeros((128, TOK), F32))
    vbuf[c, 0:128] = h0
    ch0 = dot_right(cc, h0) * grow_full
    cb_ch0[...] = ch0
    y = ycur[...] + ch0 + skip_in[...] * xf
    ycur[...] = y
    zf = gate[...].astype(F32)
    sig = 1.0 / (1.0 + jnp.exp(-zf))
    gated = y * zf * sig
    squares = dot_high(jnp.ones((8, TOK), F32), gated * gated, 1, 1)
    gsum_b[v % 4] = squares[0:1]
    gsum_x.start(v % 4)

    for n, h in enumerate((far, near)):
        rs_wait(from_m.at[n], 4 + n)
        rs_wait(from_p.at[n], 6 + n)
        for j in range(4):
            i = 4 * (2 * x + h) + j
            total = pbuf[i].astype(F32) + from_m[n, j].astype(F32) + from_p[n, j].astype(F32)
            pbuf[i] = total.astype(BF16)
        if n == 0:
            for j in range(4):
                zz = 4 * h + j
                send(pbuf.at[x * 8 + zz], rz.at[z], rs_s.at[8], rs_r.at[8], {"vocab": x * 8 + zz})
        else:
            for d in range(1, 4):
                zz = 4 * h + (z % 4 + d) % 4
                send(pbuf.at[x * 8 + zz], rz.at[z], rs_s.at[8], rs_r.at[8], {"vocab": x * 8 + zz})
    rz[z] = pbuf[v]
    grads.middle()
    outs_w.end()
    inner_x.got()
    inner = column(jnp.sum(inner_b[...], axis=0)[0:1])
    mean_x.got()
    extra = dot_high(inner_b[:, 1, :], mean_b[:, 0, :], 0, 0)
    resid_f = sbuf[v].astype(F32)
    less = resid_f * (inv * inv * inner * (1.0 / D))
    gsum_x.got()
    sums = jnp.sum(gsum_b[...], axis=0)
    ginv = column(lax.rsqrt(sums * (1.0 / (INNER // GROUPS)) + EPS))
    ginv = wide(ginv, TOK)
    ng = norm_gain[...]
    normed_t = (gated * ginv * ng).astype(BF16).T

    rs_wait(rz.at[pl.ds(0, 7)], 8)
    total = extra
    for j in range(8):
        total = total + rz[j].astype(F32)
    mine = (inv * (total * gain[v]) - less).astype(BF16)
    gr_o[...] = mine
    gbuf[v] = mine
    back.start()
    back.spread()

    grads.end()
    outs_w.finish()
    grads.finish()
    norm_x.got()
    acc[...] = jnp.zeros_like(acc)

    @pl.loop(0, 4)
    def _(i):
        acc[...] += dot(ntbuf[i], gall[i])

    back.relay()

    @pl.loop(4, CTX)
    def _(i):
        acc[...] += dot(ntbuf[i], gall[i])

    gh_o[...] = acc[...].astype(BF16)
    back.finish()

    def project(i, total):
        lhs = jnp.concatenate([gbuf[4 * i + j] for j in range(4)], axis=1)
        osend[i] = dot(normed_t, lhs).astype(BF16)
        return total + dot(lhs, owbuf[i], 1, 1)

    grad_normed = lax.fori_loop(0, CTX, project, jnp.zeros((TOK, TOK), F32))
    scaled = grad_normed * ng
    dots = dot_high(jnp.ones((8, TOK), F32), gated * scaled, 1, 1)
    gdot_b[v % 4] = dots[0:1]
    gdot_x.start(v % 4)
    out_x.start(c)
    obuf[c] = osend[c]
    gdot_x.got()
    gdot = wide(column(jnp.sum(gdot_b[...], axis=0)), TOK)
    grad_gated = ginv * scaled - gated * (ginv * ginv * ginv * gdot * (1.0 / (INNER // GROUPS)))
    gg_o[...] = (grad_gated * y * sig * (1.0 + zf * (1.0 - sig))).astype(BF16)
    gy = grad_gated * zf * sig
    gyb[...] = gy
    gye = gy * grow_full
    h0 = vbuf[c, 0:128]
    dc = dot_both(gye, h0, 1, 1)
    vbuf[c, 0:128] = dot_right(cc, gye, 0, 0)
    vbuf[c, 128:STATE_ROWS] = jnp.zeros((STATE_ROWS - 128, TOK), F32)
    adjoints.start()

    ones8 = jnp.ones((8, TOK), F32)
    dcb = jnp.zeros((TOK, TOK), F32)
    rows_m, cols_m = [], []
    for h in range(4):
        if h == 2:
            adjoints.middle()
        pair = h // 2
        gyp = gyb[:, pair * 128 : pair * 128 + 128]
        gym = jnp.where(low if h % 2 == 0 else jnp.logical_not(low), gyp, 0.0)
        e = es[h]
        s = cbb[...] * e
        ds = dot_left(gym, xb[:, pair * 128 : pair * 128 + 128], 1, 1)
        dcb = dcb + ds * e
        m = ds * s
        rows_m.append(dot_high(ones8, m, 1, 1)[0:1])
        cols_m.append(jnp.sum(m, axis=0, keepdims=True))
        part = dot_both(s, gym, 0, 0)
        if h % 2 == 0:
            held = part
        else:
            logits[:, pair * 128 : pair * 128 + 128] = held + part
    adjoints.end()
    zero4 = jnp.zeros((4, TOK), F32)
    rows_m = jnp.concatenate(rows_m + [zero4], axis=0)
    cols_m = jnp.concatenate(cols_m + [zero4], axis=0)
    dc = dc + dot_left(dcb, b)
    db = dot_left(dcb, cc, 0, 0)
    r_rows = dot_high(sel, gy * cb_ch0[...], 1, 1)
    adjoints.finish()

    def leave(j, h1):
        i = CTX - 1 - j
        new = ubuf[i, 128:129] * h1 + vbuf[i, 0:128]
        return jnp.where(i > c, new, h1)

    h1 = lax.fori_loop(0, CTX - 1, leave, jnp.zeros((128, TOK), F32))
    bdh = dot_right(b, h1) * tail_full
    gx_o[...] = (logits[:, 0:TOK] + skip_in[...] * gy + bdh).astype(BF16)
    db = db + dot_both(tail_full * xf, h1, 1, 1)
    bcs[:, 0] = db.reshape(VOC, 8, 128)
    bcs[:, 1] = dc.reshape(VOC, 8, 128)
    bcr[v] = bcs[v]
    bc_x.start(v)
    wq = dot_high(sel, bdh * xf, 1, 1)

    def again(j, h0):
        new = ubuf[j, 128:129] * h0 + ubuf[j, 0:128]
        return jnp.where(j < c, new, h0)

    h0 = lax.fori_loop(0, CTX - 1, again, jnp.zeros((128, TOK), F32))
    cross = jnp.sum(h0 * h1, axis=0, keepdims=True) * ubuf[c, 128:129]
    cross = dot_high(sel, jnp.broadcast_to(cross, (8, TOK)), 1, 1)[:, 0:1]
    gdt_o[...] = (cols_m + wq) / dt
    da = rows_m - cols_m + r_rows - wq
    at_end = cross + jnp.sum(wq, axis=1, keepdims=True)
    gld_o[...] = dot_high(da, (row_i >= col_i).astype(F32)) + at_end

    bc_x.got()
    for n, out in enumerate((gb_o, gc_o)):
        parts = []
        for g in range(GROUPS):
            parts.append((bcr[4 * g, n] + bcr[4 * g + 1, n]) + (bcr[4 * g + 2, n] + bcr[4 * g + 3, n]))
        out[...] = jnp.concatenate(parts, axis=1).astype(BF16)
    out_x.got()
    for j in range(4):
        cols = pl.ds(128 * j, 128)
        total = obuf[0, :, cols].astype(F32)
        for i in range(1, CTX):
            total = total + obuf[i, :, cols].astype(F32)
        gow_o[:, cols] = total.astype(BF16)

    for gather in (weights, outs_w, grads, states, adjoints):
        gather.drain()
    stream.drain()
    back.drain()
    for many in (lse_x, inner_x, gsum_x, gdot_x, norm_x, out_x, bc_x, mean_x):
        many.drain()
    for n in range(2):
        rs_wait(rel_a.at[n], n, False)
        rs_wait(rel_b.at[n], 2 + n, False)
        rs_wait(from_m.at[n], 4 + n, False)
        rs_wait(from_p.at[n], 6 + n, False)
    rs_wait(rz.at[pl.ds(0, 7)], 8, False)


def shards(resid, gain, head_w, targets, out_w, norm_gain, xs, gate, b, c, dt, decay, skip):
    heads = skip.shape[0]
    pad = lambda rows, fill: jnp.pad(rows, ((0, 8 - heads), (0, 0)), constant_values=fill)
    args = (
        resid,
        gain.reshape(VOC, 1, 128),
        head_w,
        targets.astype(F32).reshape(1, TOK),
        out_w,
        norm_gain.reshape(1, TOK),
        xs,
        gate,
        b,
        c,
        pad(dt, 1.0),
        pad(decay, 0.0),
        jnp.repeat(skip, TOK // heads).reshape(1, TOK),
    )
    vm = pl.BlockSpec(memory_space=pltpu.VMEM)
    hbm = pl.BlockSpec(memory_space=pl.ANY)
    shape = jax.ShapeDtypeStruct
    dma = pltpu.SemaphoreType.DMA
    scratch = [
        pltpu.VMEM((CTX, 512, 1024), BF16),
        pltpu.VMEM((CTX, TOK, 512), BF16),
        pltpu.VMEM((VOC, TOK, 128), BF16),
        pltpu.VMEM((CTX, TOK, 512), BF16),
        pltpu.VMEM((CTX, 512, TOK), BF16),
        pltpu.VMEM((CTX, 512, TOK), BF16),
        pltpu.VMEM((TOK, 1024), F32),
        pltpu.VMEM((CTX, TOK, 1024), BF16),
        pltpu.VMEM((VOC, TOK, 128), BF16),
        pltpu.VMEM((2, 4, HALF, 128), BF16),
        pltpu.VMEM((2, 4, HALF, 128), BF16),
        pltpu.VMEM((2, 4, TOK, 128), BF16),
        pltpu.VMEM((2, 4, TOK, 128), BF16),
        pltpu.VMEM((8, TOK, 128), BF16),
        pltpu.VMEM((VOC, TOK, 128), BF16),
        pltpu.VMEM((CTX, STATE_ROWS, TOK), F32),
        pltpu.VMEM((CTX, STATE_ROWS, TOK), F32),
        pltpu.VMEM((CTX, TOK, 512), BF16),
        pltpu.VMEM((CTX, TOK, 512), BF16),
        pltpu.VMEM((4, TOK, TOK), F32),
        pltpu.VMEM((512, 1024), F32),
        pltpu.VMEM((VOC, 1, TOK), F32),
        pltpu.VMEM((VOC, 2, TOK), F32),
        pltpu.VMEM((4, 1, TOK), F32),
        pltpu.VMEM((4, 1, TOK), F32),
        pltpu.VMEM((VOC, 1, 128), F32),
        pltpu.VMEM((VOC, 1, 128), F32),
        pltpu.VMEM((VOC, 2, 8, 128), F32),
        pltpu.VMEM((VOC, 2, 8, 128), F32),
        pltpu.VMEM((TOK, 128), F32),
        pltpu.VMEM((TOK, TOK), F32),
        pltpu.VMEM((TOK, TOK), F32),
        pltpu.VMEM((TOK, TOK), F32),
        pltpu.VMEM((TOK, TOK), F32),
        dma((3,)),
        dma((9,)), dma((9,)), dma((9,)), dma((9,)), dma((9,)), dma((9,)), dma((9,)), dma((9,)), dma((9,)), dma((9,)),
        dma((5,)), dma((40,)), dma((5,)), dma((40,)),
        dma((9,)), dma((9,)),
        dma((8,)), dma((8,)),
    ]
    outs = pl.pallas_call(
        kernel,
        out_shape=(
            shape((512, 1024), BF16),
            shape((TOK, 128), BF16),
            shape((TOK, 512), BF16),
            shape((TOK, TOK), BF16),
            shape((TOK, TOK), BF16),
            shape((8, 1024), BF16),
            shape((8, 1024), BF16),
            shape((8, TOK), F32),
            shape((8, TOK), F32),
        ),
        in_specs=[hbm, vm, hbm, vm, hbm] + [vm] * 8,
        out_specs=(vm,) * 9,
        scratch_shapes=scratch,
        compiler_params=pltpu.CompilerParams(
            collective_id=0, has_side_effects=True, vmem_limit_bytes=67043328
        ),
        name="step",
    )(*args)
    return outs[:7] + (outs[7][:heads], outs[8][:heads])


def solution(mesh):
    return jax.shard_map(
        shards,
        mesh=mesh,
        in_specs=(
            P("ctx", "vocab"),
            P(),
            P("ctx", "vocab"),
            P("ctx"),
            P("vocab", "ctx"),
            P("vocab"),
            P("ctx", "vocab"),
            P("ctx", "vocab"),
            P("ctx", None),
            P("ctx", None),
            P("vocab", "ctx"),
            P("vocab", "ctx"),
            P("vocab"),
        ),
        out_specs=(
            P("ctx", "vocab"),
            P("ctx", "vocab"),
            P("vocab", "ctx"),
            P("ctx", "vocab"),
            P("ctx", "vocab"),
            P(("ctx", "vocab"), None),
            P(("ctx", "vocab"), None),
            P("vocab", "ctx"),
            P("vocab", "ctx"),
        ),
        check_vma=False,
    )
```

time: 1460 us -> 201 us (0.14)
  waiting for transfers between devices: 980 us -> 0 us
  blocking collectives: 330 us -> 0 us
  Pallas kernels: 0 us -> 188 us
  matrix products: 62 us -> 0 us
  local copies, waits for them, and re-layouts: 50.9 us -> 11.6 us
  other arithmetic: 23.7 us -> 0.56 us
    reduce_scatter x5 -> x0, waiting for transfers between devices: 737 us -> none  [the longest x1 218 us: shards(): lax.psum_scatter(grad_c_float, 'vocab', scatter_dimension=0, tiled=True)]
    all_gather x6 -> x0, waiting for transfers between devices: 241 us -> none  [the longest x1 69.4 us: shards(): stream = lax.all_gather(resid_out, 'vocab', axis=1, tiled=True)]
    psum x3 -> x0, blocking collectives: 229 us -> none  [the longest x1 114 us: shards(): lax.psum(jnp.dot(jnp.sum(gated_heads * gated_heads, axis=2), selector, pr...]
    pallas_call x0 -> x1, Pallas kernels: none -> 188 us  [shards(): pl.pallas_call(kernel, out_shape=(shape((512, 1024), BF16), shape((TOK, 1...]
    dot_general x39 -> x0, matrix products: 62 us -> none  [the longest x1 8.35 us: shards(): lax.dot_general(columns, grad_logits, (((0,), (0,)), ((), ())), preferred...]
    pmax x1 -> x0, blocking collectives: 61.2 us -> none  [shards(): row_max = lax.pmax(local_max, 'vocab')]
    unnamed x1 -> x0, blocking collectives: 40.1 us -> none
    dynamic_slice x47 -> x0, local copies, waits for them, and re-layouts: 23.6 us -> none  [the longest x32 16.8 us: hop(): new = combine(before, jax.tree.map(lambda part: part[at], everything))]
  transfers between devices with their start and end apart: 11 -> 0, of which waited for: 9 -> 0; matrix products, arithmetic and copies ran while one was open for 5% -> 0% of each run, Pallas kernels for 0% -> 0%
where the time goes in v1:
time: 201 us; the launch traced here: 200 us
  Pallas kernels  188 us (94%)
  local copies, waits for them, and re-layouts  11.6 us (6%)
    pallas_call x1, Pallas kernels, shards(): pl.pallas_call(kernel, out_shape=(shape((512, 1024), BF16), shape((TOK, 1...  188 us
    unnamed x31, local copies, waits for them, and re-layouts  8.48 us

profile of v1, /device:TPU:1, one launch (start us, length us, event | category | flops | bytes accessed | tf_op | source)
XLA Modules:
  0.0 200.5 jit_solution(14972008650523144195)
XLA Ops:
  0.6 0.0 copy-start.10
  0.7 0.7 copy-done.10
  1.3 0.0 copy-start.11
  1.3 0.6 convert_element_type.3
  1.9 0.0 copy-start.6
  1.9 0.1 copy-done.11
  2.0 0.1 broadcast_in_dim.3
  2.0 0.6 reshape_reshape.3.refs_12_
  2.7 0.0 copy-done.6
  2.7 0.0 copy-start.7
  2.7 0.6 pad.7.refs_10_
  3.3 0.1 copy-done.7
  3.4 0.6 pad.8.refs_11_
  4.0 187.6 %step.1 = (bf16[512,1024]{1,0:T(8,128)(2,1)}, bf16[256,128]{1,0:T(8,128)(2,1)}, bf16[256,512]{1,0:T(8,128)(2,1)}, bf16[256,256]{1,0:T(8,128)(2,1)}, bf16[256,256...) custom-call(bf16[256,128]{1,0:T(8,128)(2,1)} %refs_0_.1, ...), custom_call_target="tpu_custom_call" | custom-call | tf_op jit(solution)/shard_map/step/pallas_call | solution.py:708
  191.6 0.0 copy-start.9
  191.6 0.0 copy-start.8
  191.6 0.7 copy-done.9
  192.3 0.6 slice.6
  192.9 0.0 copy-done.8
  192.9 0.6 slice.7
  193.5 0.0 copy-start.3
  193.5 0.0 copy-start
  193.5 2.3 %copy.29 = bf16[512,1024]{1,0:T(8,128)(2,1)} copy(bf16[512,1024]{1,0:T(8,128)(2,1)} %get-tuple-element.36) | data formatting | bytes 2097152
  195.8 0.0 copy-done.3
  195.8 0.6 copy.30
  196.5 0.0 copy-done
  196.5 0.0 copy-start.2
  196.5 0.7 copy.31
  197.2 0.3 copy-done.2
  197.5 0.0 copy-start.1
  197.5 0.7 copy.32
  198.1 0.3 copy-done.1
  198.4 0.0 copy-start.5
  198.4 0.7 copy.33
  199.1 0.1 copy-done.5
  199.1 0.0 copy-start.4
  199.1 0.6 copy.34
  199.7 0.1 copy-done.4
  199.9 0.6 copy.35
Async XLA Ops:
  0.6 0.7 copy-start.10
  1.3 0.7 copy-start.11
  1.9 0.8 copy-start.6
  2.7 0.7 copy-start.7
  191.6 0.7 copy-start.9
  191.6 1.3 copy-start.8
  193.5 2.3 %copy-start.3 = (bf16[256,128]{1,0:T(8,128)(2,1)S(1)}, bf16[256,128]{1,0:T(8,128)(2,1)}, u32[]{:S(2)}) copy-start(bf16[256,128]{1,0:T(8,128)(2,1)} %get-tuple-element.37) | copy-start | bytes 196612
  193.5 2.9 %copy-start = (bf16[256,512]{1,0:T(8,128)(2,1)S(1)}, bf16[256,512]{1,0:T(8,128)(2,1)}, u32[]{:S(2)}) copy-start(bf16[256,512]{1,0:T(8,128)(2,1)} %get-tuple-element.38) | copy-start | bytes 786436
  196.5 1.0 copy-start.2
  197.5 1.0 copy-start.1
  198.4 0.7 copy-start.5
  199.1 0.7 copy-start.4

commit v2 on v1

--- a/solution.py
+++ b/solution.py
@@ -104,16 +104,20 @@
         ).wait_send()
 
     def start(self):
-        self.go(0, self.own, self.yp)
-        self.go(1, self.own, self.ym)
+        self.go(0, self.own, self.yp, self.top)
+        self.go(1, self.own, self.ym, self.bottom)
+        self.go(9, self.own, self.yp, self.bottom)
+        self.go(10, self.own, self.ym, self.top)
         self.go(2, self.own, self.sib)
 
     def middle(self):
-        self.got(0, self.ym)
+        self.got(0, self.ym, self.top)
         self.go(5, self.ym, self.yp, self.top)
+        self.got(1, self.yp, self.bottom)
+        self.go(6, self.yp, self.ym, self.bottom)
+        self.got(9, self.ym, self.bottom)
         self.go(3, self.ym, self.sib)
-        self.got(1, self.yp)
-        self.go(6, self.yp, self.ym, self.bottom)
+        self.got(10, self.yp, self.top)
         self.go(4, self.yp, self.sib)
 
     def end(self):
@@ -133,8 +137,10 @@
         self.got(8, self.sy2, self.bottom)
 
     def drain(self):
-        self.sent(0, self.own)
-        self.sent(1, self.own)
+        self.sent(0, self.own, self.top)
+        self.sent(1, self.own, self.bottom)
+        self.sent(9, self.own, self.bottom)
+        self.sent(10, self.own, self.top)
         self.sent(2, self.own)
         self.sent(3, self.ym)
         self.sent(4, self.yp)
@@ -145,6 +151,7 @@
 
 
 ORDER = (0, 1, 7, 2, 6, 3, 5, 4)
+LAG = 3
 
 
 class Voc:
@@ -169,25 +176,34 @@
             ref = self.buf.at[self.v]
             send(ref, ref, self.s.at[0], self.r.at[d], {"vocab": self.x * 8 + (self.z + d) % 8})
 
-    def spread(self):
-        for d in ORDER:
-            ref = self.buf.at[self.x * 8 + (self.z + 8 - d) % 8]
-            if d:
-                self.wait(ref, self.s.at[0], self.r.at[d], True)
-            send(ref, ref, self.s.at[1], self.r.at[8 + d], {"vocab": self.xp * 8 + self.z})
-            send(ref, ref, self.s.at[2], self.r.at[16 + d], {"vocab": self.xm * 8 + self.z})
+    def forward(self, d):
+        ref = self.buf.at[self.x * 8 + (self.z + 8 - d) % 8]
+        if d:
+            self.wait(ref, self.s.at[0], self.r.at[d], True)
+        send(ref, ref, self.s.at[1], self.r.at[8 + d], {"vocab": self.xp * 8 + self.z})
+        send(ref, ref, self.s.at[2], self.r.at[16 + d], {"vocab": self.xm * 8 + self.z})
+
+    def pass_on(self, d):
+        zz = (self.z + 8 - d) % 8
+        block = self.xm * 8 + zz
+        self.wait(self.buf.at[block], self.s.at[1], self.r.at[8 + d], True)
+        ref = self.buf.at[block, pl.ds(0, HALF)]
+        send(ref, ref, self.s.at[3], self.r.at[24 + d], {"vocab": self.xp * 8 + self.z})
+        block = self.xp * 8 + zz
+        self.wait(self.buf.at[block], self.s.at[2], self.r.at[16 + d], True)
+        ref = self.buf.at[block, pl.ds(HALF, HALF)]
+        send(ref, ref, self.s.at[4], self.r.at[32 + d], {"vocab": self.xm * 8 + self.z})
+
+    def spread(self, first=0):
+        for n in range(8):
+            if n >= first:
+                self.forward(ORDER[n])
+            if n >= LAG:
+                self.pass_on(ORDER[n - LAG])
 
     def relay(self):
-        for d in ORDER:
-            zz = (self.z + 8 - d) % 8
-            block = self.xm * 8 + zz
-            self.wait(self.buf.at[block], self.s.at[1], self.r.at[8 + d], True)
-            ref = self.buf.at[block, pl.ds(0, HALF)]
-            send(ref, ref, self.s.at[3], self.r.at[24 + d], {"vocab": self.xp * 8 + self.z})
-            block = self.xp * 8 + zz
-            self.wait(self.buf.at[block], self.s.at[2], self.r.at[16 + d], True)
-            ref = self.buf.at[block, pl.ds(HALF, HALF)]
-            send(ref, ref, self.s.at[4], self.r.at[32 + d], {"vocab": self.xm * 8 + self.z})
+        for n in range(8 - LAG, 8):
+            self.pass_on(ORDER[n])
 
     def finish(self):
         for d in ORDER:
@@ -230,15 +246,16 @@
 
 def kernel(*refs):
     (resid, gain, head_w, target, out_w, norm_gain, xs, gate, b_in, c_in, dt_in, decay_in, skip_in) = refs[:13]
-    (gh_o, gr_o, gow_o, gx_o, gg_o, gb_o, gc_o, gdt_o, gld_o) = refs[13:22]
+    (gh_h, gr_h, gow_h, gx_h, gg_h, gb_o, gc_o, gdt_o, gld_o) = refs[13:22]
     (wbuf, owbuf, sbuf, nbuf, ntsend, ntbuf, logits, gall, pbuf, rel_a, rel_b, from_m, from_p, rz, gbuf,
-     ubuf, vbuf, osend, obuf, es, acc, lse_b, inner_b, gsum_b, gdot_b, mean_s, mean_b, bcs, bcr, mcol, ycur, cbb, cb_ch0, gyb,
-     lsem, ws, wr, ows, owr, gs, gr, us, ur, vs, vr, s1s, s1r, s2s, s2r, rs_s, rs_r, ms, mr) = refs[22:]
+     ubuf, vbuf, osend, obuf, es, acc, lse_b, inner_b, gsum_b, gdot_b, mean_s, mean_b, b_send, b_got, c_send, c_got, orel, xs_v, gate_v, b_v, c_v, gh_o, gr_o, gow_o, gx_o, gg_o, mcol, ycur, cbb, cb_ch0, gyb,
+     lsem, ws, wr, ows, owr, gs, gr, us, ur, vs, vr, s1s, s1r, s2s, s2r, rs_s, rs_r, ms, mr, os_s, os_r) = refs[22:]
     c = lax.axis_index("ctx")
     v = lax.axis_index("vocab")
     x, z = v // 8, v % 8
     xp, xm, x2 = (x + 1) % 4, (x + 3) % 4, (x + 2) % 4
 
+    lanes = pl.ds(pl.multiple_of((v // 4) * 128, 128), 128)
     barrier = pltpu.get_barrier_semaphore()
 
     @pl.loop(1, VOC)
@@ -253,10 +270,14 @@
         pltpu.make_async_copy(resid, sbuf.at[v], lsem.at[0]),
         pltpu.make_async_copy(head_w, wbuf.at[c], lsem.at[1]),
         pltpu.make_async_copy(out_w, owbuf.at[c], lsem.at[2]),
+        pltpu.make_async_copy(xs, xs_v, lsem.at[3]),
+        pltpu.make_async_copy(gate, gate_v, lsem.at[4]),
+        pltpu.make_async_copy(b_in.at[:, lanes], b_v, lsem.at[5]),
+        pltpu.make_async_copy(c_in.at[:, lanes], c_v, lsem.at[6]),
     ]
     for copy in local:
         copy.start()
-    for copy in local:
+    for copy in local[:2]:
         copy.wait()
     pl.semaphore_wait(barrier, VOC + CTX - 2)
 
@@ -276,31 +297,41 @@
     gsum_x = Many("vocab", v, over_g, 4, lambda to: gsum_b.at[v % 4], gsum_b, ms.at[2], mr.at[2])
     gdot_x = Many("vocab", v, over_g, 4, lambda to: gdot_b.at[v % 4], gdot_b, ms.at[3], mr.at[3])
     norm_x = Many("ctx", c, over_c, CTX, lambda to: ntsend.at[to], ntbuf, ms.at[4], mr.at[4])
-    out_x = Many("ctx", c, over_c, CTX, lambda to: osend.at[to], obuf, ms.at[5], mr.at[5])
-    bc_x = Many("vocab", v, over_v, VOC, lambda to: bcs.at[to], bcr, ms.at[6], mr.at[6])
+    b_x = Many("vocab", v, over_v, VOC, lambda to: b_send.at[to], b_got, ms.at[6], mr.at[6])
+    c_x = Many("vocab", v, over_v, VOC, lambda to: c_send.at[to], c_got, ms.at[5], mr.at[5])
     mean_x = Many("vocab", v, over_v, VOC, lambda to: mean_s.at[to], mean_b, ms.at[7], mr.at[7])
 
+    puts = [
+        pltpu.make_async_copy(src, dst, lsem.at[7 + n])
+        for n, (src, dst) in enumerate(
+            ((gh_o, gh_h), (gr_o, gr_h), (gow_o, gow_h), (gx_o, gx_h), (gg_o, gg_h))
+        )
+    ]
     stream.start()
     weights.start()
     stream.spread()
 
-    group = v // 4
-    lanes = pl.ds(pl.multiple_of(group * 128, 128), 128)
-    b = b_in[:, lanes]
-    cc = c_in[:, lanes]
-    xb = xs[...]
+    for copy in local[2:]:
+        copy.wait()
+    b = b_v[...]
+    cc = c_v[...]
+    xb = xs_v[...]
     xf = xb.astype(F32)
     row_i = lax.broadcasted_iota(jnp.int32, (TOK, TOK), 0)
     col_i = lax.broadcasted_iota(jnp.int32, (TOK, TOK), 1)
     upper = (row_i <= col_i).astype(F32)
     head_of = lax.broadcasted_iota(jnp.int32, (8, TOK), 1) // 64
     sel = (head_of == lax.broadcasted_iota(jnp.int32, (8, TOK), 0)).astype(F32)
-    dt = dt_in[...]
-    a = dot_high(decay_in[...], upper)
+    dt = jnp.concatenate([dt_in[...], jnp.ones((4, TOK), F32)], axis=0)
+    decay = jnp.concatenate([decay_in[...], jnp.zeros((4, TOK), F32)], axis=0)
+    a = dot_high(decay, upper)
     last = a[:, TOK - 1 :]
     tail = jnp.exp(last - a) * dt
     a_cols = jnp.concatenate([a] * 16, axis=0).T
     cbb[...] = dot(cc, b, 1, 1)
+    skip = jnp.zeros((1, TOK), F32)
+    for h in range(4):
+        skip = skip + sel[h : h + 1] * skip_in[h]
     low = lax.broadcasted_iota(jnp.int32, (TOK, 128), 1) < 64
     for pair in range(2):
         outs = []
@@ -362,7 +393,6 @@
 
     states.start()
     outs_w.start()
-    norm_x.start(c)
 
     @pl.loop(0, 4)
     def _(i):
@@ -374,8 +404,7 @@
 
     lse_b[v] = row_of(mcol[...])
     lse_x.start(v)
-    target_col = column(target[...])
-    states.middle()
+    target_col = column(target[...].astype(F32))
     lse_x.got()
     every = lse_b[...]
     most = jnp.max(every, axis=0)
@@ -402,6 +431,8 @@
     inner_b[v, 1:2] = row_of(cb_ch0[:, 128:256])
     inner_x.start(v)
 
+    top, bottom = pl.ds(0, HALF), pl.ds(HALF, HALF)
+
     weigh = jnp.concatenate([gall[c], jnp.full((16, 1024), 2.0**-10, BF16)], axis=0)
     sums_g = cb_ch0[:, 128:256]
 
@@ -412,129 +443,116 @@
             mean_s[4 * i + j] = mean
             pbuf[4 * i + j] = (part[0:TOK, j * 128 : j * 128 + 128] - sums_g * mean).astype(BF16)
 
-    rs = lambda i: (rs_s.at[i], rs_r.at[i])
     to_p, to_m = {"vocab": xp * 8 + z}, {"vocab": xm * 8 + z}
 
-    def rs_wait(ref, i, receive=True):
+    def rs_send(kind, n, src, dst, to):
+        send(src, dst, rs_s.at[kind], rs_r.at[8 * kind + n], to)
+
+    def rs_wait(kind, n, ref, receive=True):
         copy = pltpu.make_async_remote_copy(
-            src_ref=ref, dst_ref=ref, send_sem=rs_s.at[i], recv_sem=rs_r.at[i], device_id=to_p, device_id_type=MESH
+            src_ref=ref, dst_ref=ref, send_sem=rs_s.at[kind], recv_sem=rs_r.at[8 * kind + n],
+            device_id=to_p, device_id_type=MESH,
         )
         if receive:
             copy.wait_recv()
         else:
             copy.wait_send()
 
-    top, bottom = pl.ds(0, HALF), pl.ds(HALF, HALF)
     far, near = 1 - z // 4, z // 4
-    for n, h in enumerate((far, near)):
-        partial(2 * x2 + h)
-        four = pl.ds(4 * (2 * x2 + h), 4)
-        send(pbuf.at[four, top], rel_a.at[n], *rs(n), to_p)
-        send(pbuf.at[four, bottom], rel_b.at[n], *rs(2 + n), to_m)
+    serve = [4 * far + (z % 4 + 1 + j) % 4 for j in range(4)] + [4 * near + (z % 4 + 1 + j) % 4 for j in range(4)]
+    for n in range(8):
+        if n % 4 == 0:
+            partial(2 * x2 + (far, near)[n // 4])
+        rs_send(0, n, pbuf.at[x2 * 8 + serve[n], top], rel_a.at[n], to_p)
+        rs_send(1, n, pbuf.at[x2 * 8 + serve[n], bottom], rel_b.at[n], to_m)
     grads.start()
-    for n, h in enumerate((far, near)):
+    for h in (far, near):
         partial(2 * xp + h)
         partial(2 * xm + h)
-    for n, h in enumerate((far, near)):
+
+    def relayed(n):
+        rs_wait(0, n, rel_a.at[n])
+        i = xp * 8 + serve[n]
+        pbuf[i, 0:HALF] = (pbuf[i, 0:HALF].astype(F32) + rel_a[n].astype(F32)).astype(BF16)
+        rs_send(2, n, pbuf.at[i], from_m.at[n], to_p)
+        rs_wait(1, n, rel_b.at[n])
+        i = xm * 8 + serve[n]
+        pbuf[i, HALF:TOK] = (pbuf[i, HALF:TOK].astype(F32) + rel_b[n].astype(F32)).astype(BF16)
+        rs_send(3, n, pbuf.at[i], from_p.at[n], to_m)
+
+    for n in range(2):
+        relayed(n)
+    for h in (far, near):
         partial(2 * x + h)
+    for n in range(2, 8):
+        relayed(n)
     mean_b[v] = mean_s[v]
     mean_x.start(v)
+    states.middle()
+    outs_w.middle()
+    norm_x.start(c)
+
+    for n in range(8):
+        rs_wait(2, n, from_m.at[n])
+        rs_wait(3, n, from_p.at[n])
+        i = x * 8 + serve[n]
+        total = pbuf[i].astype(F32) + from_m[n].astype(F32) + from_p[n].astype(F32)
+        pbuf[i] = total.astype(BF16)
+        if n < 7:
+            send(pbuf.at[i], rz.at[z], rs_s.at[4], rs_r.at[32], {"vocab": i})
+    rz[z] = pbuf[v]
     states.end()
-    outs_w.middle()
-    for n, h in enumerate((far, near)):
-        rs_wait(rel_a.at[n], n)
-        for j in range(4):
-            i = 4 * (2 * xp + h) + j
-            pbuf[i, 0:HALF] = (pbuf[i, 0:HALF].astype(F32) + rel_a[n, j].astype(F32)).astype(BF16)
-        send(pbuf.at[pl.ds(4 * (2 * xp + h), 4)], from_m.at[n], *rs(4 + n), to_p)
-        rs_wait(rel_b.at[n], 2 + n)
-        for j in range(4):
-            i = 4 * (2 * xm + h) + j
-            pbuf[i, HALF:TOK] = (pbuf[i, HALF:TOK].astype(F32) + rel_b[n, j].astype(F32)).astype(BF16)
-        send(pbuf.at[pl.ds(4 * (2 * xm + h), 4)], from_p.at[n], *rs(6 + n), to_m)
-
-    states.finish()
-
-    def enter(j, h0):
-        new = ubuf[j, 128:129] * h0 + ubuf[j, 0:128]
-        return jnp.where(j < c, new, h0)
-
-    h0 = lax.fori_loop(0, CTX - 1, enter, jnp.zeros((128, TOK), F32))
-    vbuf[c, 0:128] = h0
-    ch0 = dot_right(cc, h0) * grow_full
-    cb_ch0[...] = ch0
-    y = ycur[...] + ch0 + skip_in[...] * xf
-    ycur[...] = y
-    zf = gate[...].astype(F32)
-    sig = 1.0 / (1.0 + jnp.exp(-zf))
-    gated = y * zf * sig
-    squares = dot_high(jnp.ones((8, TOK), F32), gated * gated, 1, 1)
-    gsum_b[v % 4] = squares[0:1]
-    gsum_x.start(v % 4)
-
-    for n, h in enumerate((far, near)):
-        rs_wait(from_m.at[n], 4 + n)
-        rs_wait(from_p.at[n], 6 + n)
-        for j in range(4):
-            i = 4 * (2 * x + h) + j
-            total = pbuf[i].astype(F32) + from_m[n, j].astype(F32) + from_p[n, j].astype(F32)
-            pbuf[i] = total.astype(BF16)
-        if n == 0:
-            for j in range(4):
-                zz = 4 * h + j
-                send(pbuf.at[x * 8 + zz], rz.at[z], rs_s.at[8], rs_r.at[8], {"vocab": x * 8 + zz})
-        else:
-            for d in range(1, 4):
-                zz = 4 * h + (z % 4 + d) % 4
-                send(pbuf.at[x * 8 + zz], rz.at[z], rs_s.at[8], rs_r.at[8], {"vocab": x * 8 + zz})
-    rz[z] = pbuf[v]
-    grads.middle()
     outs_w.end()
+
     inner_x.got()
     inner = column(jnp.sum(inner_b[...], axis=0)[0:1])
     mean_x.got()
     extra = dot_high(inner_b[:, 1, :], mean_b[:, 0, :], 0, 0)
     resid_f = sbuf[v].astype(F32)
     less = resid_f * (inv * inv * inner * (1.0 / D))
+    rs_wait(4, 0, rz.at[pl.ds(0, 7)])
+    total = extra
+    for j in range(8):
+        total = total + rz[j].astype(F32)
+    mine = (inv * (total * gain[v]) - less).astype(BF16)
+    gr_o[...] = mine
+    puts[1].start()
+    gbuf[v] = mine
+    back.start()
+    back.forward(0)
+    states.finish()
+
+    def enter(j, h0):
+        new = ubuf[j, 128:129] * h0 + ubuf[j, 0:128]
+        return jnp.where(j < c, new, h0)
+
+    h0 = lax.fori_loop(0, CTX - 1, enter, jnp.zeros((128, TOK), F32))
+    vbuf[c, 0:128] = h0
+    ch0 = dot_right(cc, h0) * grow_full
+    cb_ch0[...] = ch0
+    y = ycur[...] + ch0 + skip * xf
+    ycur[...] = y
+    zf = gate_v[...].astype(F32)
+    sig = 1.0 / (1.0 + jnp.exp(-zf))
+    gated = y * zf * sig
+    squares = dot_high(jnp.ones((8, TOK), F32), gated * gated, 1, 1)
+    gsum_b[v % 4] = squares[0:1]
+    gsum_x.start(v % 4)
+
+    back.spread(1)
+    back.relay()
     gsum_x.got()
     sums = jnp.sum(gsum_b[...], axis=0)
     ginv = column(lax.rsqrt(sums * (1.0 / (INNER // GROUPS)) + EPS))
     ginv = wide(ginv, TOK)
     ng = norm_gain[...]
     normed_t = (gated * ginv * ng).astype(BF16).T
-
-    rs_wait(rz.at[pl.ds(0, 7)], 8)
-    total = extra
-    for j in range(8):
-        total = total + rz[j].astype(F32)
-    mine = (inv * (total * gain[v]) - less).astype(BF16)
-    gr_o[...] = mine
-    gbuf[v] = mine
-    back.start()
-    back.spread()
-
-    grads.end()
     outs_w.finish()
-    grads.finish()
-    norm_x.got()
-    acc[...] = jnp.zeros_like(acc)
-
-    @pl.loop(0, 4)
-    def _(i):
-        acc[...] += dot(ntbuf[i], gall[i])
-
-    back.relay()
-
-    @pl.loop(4, CTX)
-    def _(i):
-        acc[...] += dot(ntbuf[i], gall[i])
-
-    gh_o[...] = acc[...].astype(BF16)
+    grads.middle()
     back.finish()
 
     def project(i, total):
         lhs = jnp.concatenate([gbuf[4 * i + j] for j in range(4)], axis=1)
-        osend[i] = dot(normed_t, lhs).astype(BF16)
         return total + dot(lhs, owbuf[i], 1, 1)
 
     grad_normed = lax.fori_loop(0, CTX, project, jnp.zeros((TOK, TOK), F32))
@@ -542,14 +560,36 @@
     dots = dot_high(jnp.ones((8, TOK), F32), gated * scaled, 1, 1)
     gdot_b[v % 4] = dots[0:1]
     gdot_x.start(v % 4)
-    out_x.start(c)
-    obuf[c] = osend[c]
+
+    @pl.loop(0, CTX)
+    def _(i):
+        lhs = jnp.concatenate([gbuf[4 * i + j] for j in range(4)], axis=1)
+        osend[(i % 2) * 4 + i // 2] = dot(normed_t, lhs).astype(BF16)
+
+    y_at, k_at = c // 2, c % 2
+    side, c_p, c_m = y_at * 2 + 1 - k_at, ((y_at + 1) % 4) * 2 + k_at, ((y_at + 3) % 4) * 2 + k_at
+    at_p, at_m, at_2 = k_at * 4 + (y_at + 1) % 4, k_at * 4 + (y_at + 3) % 4, k_at * 4 + (y_at + 2) % 4
+
+    def os_copy(n, src, dst, to):
+        return pltpu.make_async_remote_copy(
+            src_ref=src, dst_ref=dst, send_sem=os_s.at[n], recv_sem=os_r.at[n], device_id={"ctx": to}, device_id_type=MESH
+        )
+
+    os_copies = (
+        os_copy(0, osend.at[pl.ds((1 - k_at) * 4, 4)], obuf.at[pl.ds(0, 4)], side),
+        os_copy(1, osend.at[at_2, top], orel.at[0], c_p),
+        os_copy(2, osend.at[at_2, bottom], orel.at[1], c_m),
+        os_copy(3, osend.at[at_p], obuf.at[4], c_p),
+        os_copy(4, osend.at[at_m], obuf.at[5], c_m),
+    )
+    os_copies[0].start()
     gdot_x.got()
     gdot = wide(column(jnp.sum(gdot_b[...], axis=0)), TOK)
     grad_gated = ginv * scaled - gated * (ginv * ginv * ginv * gdot * (1.0 / (INNER // GROUPS)))
     gg_o[...] = (grad_gated * y * sig * (1.0 + zf * (1.0 - sig))).astype(BF16)
     gy = grad_gated * zf * sig
     gyb[...] = gy
+    puts[4].start()
     gye = gy * grow_full
     h0 = vbuf[c, 0:128]
     dc = dot_both(gye, h0, 1, 1)
@@ -562,7 +602,21 @@
     rows_m, cols_m = [], []
     for h in range(4):
         if h == 2:
+            os_copies[0].wait_recv()
+            for j in (2, 1, 3):
+                i = k_at * 4 + (y_at + 4 - j) % 4
+                osend[i] = (osend[i].astype(F32) + obuf[(y_at + 4 - j) % 4].astype(F32)).astype(BF16)
+                if j == 2:
+                    os_copies[1].start()
+                    os_copies[2].start()
             adjoints.middle()
+        if h == 3:
+            os_copies[1].wait_recv()
+            osend[at_p, top] = (osend[at_p, top].astype(F32) + orel[0].astype(F32)).astype(BF16)
+            os_copies[3].start()
+            os_copies[2].wait_recv()
+            osend[at_m, bottom] = (osend[at_m, bottom].astype(F32) + orel[1].astype(F32)).astype(BF16)
+            os_copies[4].start()
         pair = h // 2
         gyp = gyb[:, pair * 128 : pair * 128 + 128]
         gym = jnp.where(low if h % 2 == 0 else jnp.logical_not(low), gyp, 0.0)
@@ -578,6 +632,7 @@
             held = part
         else:
             logits[:, pair * 128 : pair * 128 + 128] = held + part
+    grads.end()
     adjoints.end()
     zero4 = jnp.zeros((4, TOK), F32)
     rows_m = jnp.concatenate(rows_m + [zero4], axis=0)
@@ -585,6 +640,19 @@
     dc = dc + dot_left(dcb, b)
     db = dot_left(dcb, cc, 0, 0)
     r_rows = dot_high(sel, gy * cb_ch0[...], 1, 1)
+    c_send[...] = dc.reshape(VOC, 8, 128).astype(BF16)
+    c_x.start(v)
+    c_got[v] = c_send[v]
+    grads.finish()
+    norm_x.got()
+    acc[...] = jnp.zeros_like(acc)
+
+    @pl.loop(0, CTX)
+    def _(i):
+        acc[...] += dot(ntbuf[i], gall[i])
+
+    gh_o[...] = acc[...].astype(BF16)
+    puts[0].start()
     adjoints.finish()
 
     def leave(j, h1):
@@ -593,13 +661,13 @@
         return jnp.where(i > c, new, h1)
 
     h1 = lax.fori_loop(0, CTX - 1, leave, jnp.zeros((128, TOK), F32))
+    db = db + dot_both(tail_full * xf, h1, 1, 1)
+    b_send[...] = db.reshape(VOC, 8, 128).astype(BF16)
+    b_x.start(v)
+    b_got[v] = b_send[v]
     bdh = dot_right(b, h1) * tail_full
-    gx_o[...] = (logits[:, 0:TOK] + skip_in[...] * gy + bdh).astype(BF16)
-    db = db + dot_both(tail_full * xf, h1, 1, 1)
-    bcs[:, 0] = db.reshape(VOC, 8, 128)
-    bcs[:, 1] = dc.reshape(VOC, 8, 128)
-    bcr[v] = bcs[v]
-    bc_x.start(v)
+    gx_o[...] = (logits[:, 0:TOK] + skip * gy + bdh).astype(BF16)
+    puts[3].start()
     wq = dot_high(sel, bdh * xf, 1, 1)
 
     def again(j, h0):
@@ -609,56 +677,89 @@
     h0 = lax.fori_loop(0, CTX - 1, again, jnp.zeros((128, TOK), F32))
     cross = jnp.sum(h0 * h1, axis=0, keepdims=True) * ubuf[c, 128:129]
     cross = dot_high(sel, jnp.broadcast_to(cross, (8, TOK)), 1, 1)[:, 0:1]
-    gdt_o[...] = (cols_m + wq) / dt
+    gdt_o[...] = ((cols_m + wq) / dt)[0:4]
     da = rows_m - cols_m + r_rows - wq
     at_end = cross + jnp.sum(wq, axis=1, keepdims=True)
-    gld_o[...] = dot_high(da, (row_i >= col_i).astype(F32)) + at_end
-
-    bc_x.got()
-    for n, out in enumerate((gb_o, gc_o)):
+    gld_o[...] = (dot_high(da, (row_i >= col_i).astype(F32)) + at_end)[0:4]
+
+    os_copies[3].wait_recv()
+    os_copies[4].wait_recv()
+    mine = k_at * 4 + y_at
+    for j in range(4):
+        cols = pl.ds(128 * j, 128)
+        total = osend[mine, :, cols].astype(F32) + obuf[y_at, :, cols].astype(F32)
+        gow_o[:, cols] = (total + obuf[4, :, cols].astype(F32) + obuf[5, :, cols].astype(F32)).astype(BF16)
+    puts[2].start()
+    c_x.got()
+    b_x.got()
+    for got, out in ((b_got, gb_o), (c_got, gc_o)):
         parts = []
         for g in range(GROUPS):
-            parts.append((bcr[4 * g, n] + bcr[4 * g + 1, n]) + (bcr[4 * g + 2, n] + bcr[4 * g + 3, n]))
+            four = [got[4 * g + j].astype(F32) for j in range(4)]
+            parts.append((four[0] + four[1]) + (four[2] + four[3]))
         out[...] = jnp.concatenate(parts, axis=1).astype(BF16)
-    out_x.got()
-    for j in range(4):
-        cols = pl.ds(128 * j, 128)
-        total = obuf[0, :, cols].astype(F32)
-        for i in range(1, CTX):
-            total = total + obuf[i, :, cols].astype(F32)
-        gow_o[:, cols] = total.astype(BF16)
 
     for gather in (weights, outs_w, grads, states, adjoints):
         gather.drain()
     stream.drain()
     back.drain()
-    for many in (lse_x, inner_x, gsum_x, gdot_x, norm_x, out_x, bc_x, mean_x):
+    for many in (lse_x, inner_x, gsum_x, gdot_x, norm_x, b_x, c_x, mean_x):
         many.drain()
-    for n in range(2):
-        rs_wait(rel_a.at[n], n, False)
-        rs_wait(rel_b.at[n], 2 + n, False)
-        rs_wait(from_m.at[n], 4 + n, False)
-        rs_wait(from_p.at[n], 6 + n, False)
-    rs_wait(rz.at[pl.ds(0, 7)], 8, False)
+    rs_wait(0, 0, rel_a, False)
+    rs_wait(1, 0, rel_b, False)
+    rs_wait(2, 0, from_m, False)
+    rs_wait(3, 0, from_p, False)
+    rs_wait(4, 0, rz.at[pl.ds(0, 7)], False)
+    for copy in os_copies:
+        copy.wait_send()
+    for copy in puts:
+        copy.wait()
+
+
+def copy_kernel(*refs):
+    n = len(refs) // 3
+    ins, outs, bufs, (sin, sout) = refs[:n], refs[n : 2 * n], refs[2 * n : 3 * n], refs[3 * n :]
+    loads = [pltpu.make_async_copy(ins[i], bufs[i], sin.at[i]) for i in range(n)]
+    stores = [pltpu.make_async_copy(bufs[i], outs[i], sout.at[i]) for i in range(n)]
+    for copy in loads:
+        copy.start()
+    for load, store in zip(loads, stores):
+        load.wait()
+        store.start()
+    for store in stores:
+        store.wait()
+
+
+def hand_over(arrays):
+    n = len(arrays)
+    hbm = pl.BlockSpec(memory_space=pl.ANY)
+    return pl.pallas_call(
+        copy_kernel,
+        out_shape=tuple(jax.ShapeDtypeStruct(a.shape, a.dtype) for a in arrays),
+        in_specs=[hbm] * n,
+        out_specs=(hbm,) * n,
+        scratch_shapes=[pltpu.VMEM(a.shape, a.dtype) for a in arrays]
+        + [pltpu.SemaphoreType.DMA((n,)), pltpu.SemaphoreType.DMA((n,))],
+        name="hand_over",
+    )(*arrays)
 
 
 def shards(resid, gain, head_w, targets, out_w, norm_gain, xs, gate, b, c, dt, decay, skip):
     heads = skip.shape[0]
-    pad = lambda rows, fill: jnp.pad(rows, ((0, 8 - heads), (0, 0)), constant_values=fill)
     args = (
         resid,
         gain.reshape(VOC, 1, 128),
         head_w,
-        targets.astype(F32).reshape(1, TOK),
+        targets.reshape(1, TOK),
         out_w,
         norm_gain.reshape(1, TOK),
         xs,
         gate,
         b,
         c,
-        pad(dt, 1.0),
-        pad(decay, 0.0),
-        jnp.repeat(skip, TOK // heads).reshape(1, TOK),
+        dt,
+        decay,
+        skip,
     )
     vm = pl.BlockSpec(memory_space=pltpu.VMEM)
     hbm = pl.BlockSpec(memory_space=pl.ANY)
@@ -674,10 +775,10 @@
         pltpu.VMEM((TOK, 1024), F32),
         pltpu.VMEM((CTX, TOK, 1024), BF16),
         pltpu.VMEM((VOC, TOK, 128), BF16),
-        pltpu.VMEM((2, 4, HALF, 128), BF16),
-        pltpu.VMEM((2, 4, HALF, 128), BF16),
-        pltpu.VMEM((2, 4, TOK, 128), BF16),
-        pltpu.VMEM((2, 4, TOK, 128), BF16),
+        pltpu.VMEM((8, HALF, 128), BF16),
+        pltpu.VMEM((8, HALF, 128), BF16),
+        pltpu.VMEM((8, TOK, 128), BF16),
+        pltpu.VMEM((8, TOK, 128), BF16),
         pltpu.VMEM((8, TOK, 128), BF16),
         pltpu.VMEM((VOC, TOK, 128), BF16),
         pltpu.VMEM((CTX, STATE_ROWS, TOK), F32),
@@ -692,18 +793,31 @@
         pltpu.VMEM((4, 1, TOK), F32),
         pltpu.VMEM((VOC, 1, 128), F32),
         pltpu.VMEM((VOC, 1, 128), F32),
-        pltpu.VMEM((VOC, 2, 8, 128), F32),
-        pltpu.VMEM((VOC, 2, 8, 128), F32),
+        pltpu.VMEM((VOC, 8, 128), BF16),
+        pltpu.VMEM((VOC, 8, 128), BF16),
+        pltpu.VMEM((VOC, 8, 128), BF16),
+        pltpu.VMEM((VOC, 8, 128), BF16),
+        pltpu.VMEM((2, HALF, 512), BF16),
+        pltpu.VMEM((TOK, TOK), BF16),
+        pltpu.VMEM((TOK, TOK), BF16),
+        pltpu.VMEM((TOK, 128), BF16),
+        pltpu.VMEM((TOK, 128), BF16),
+        pltpu.VMEM((512, 1024), BF16),
+        pltpu.VMEM((TOK, 128), BF16),
+        pltpu.VMEM((TOK, 512), BF16),
+        pltpu.VMEM((TOK, TOK), BF16),
+        pltpu.VMEM((TOK, TOK), BF16),
         pltpu.VMEM((TOK, 128), F32),
         pltpu.VMEM((TOK, TOK), F32),
         pltpu.VMEM((TOK, TOK), F32),
         pltpu.VMEM((TOK, TOK), F32),
         pltpu.VMEM((TOK, TOK), F32),
-        dma((3,)),
-        dma((9,)), dma((9,)), dma((9,)), dma((9,)), dma((9,)), dma((9,)), dma((9,)), dma((9,)), dma((9,)), dma((9,)),
+        dma((12,)),
+        dma((11,)), dma((11,)), dma((11,)), dma((11,)), dma((11,)), dma((11,)), dma((11,)), dma((11,)), dma((11,)), dma((11,)),
         dma((5,)), dma((40,)), dma((5,)), dma((40,)),
-        dma((9,)), dma((9,)),
+        dma((5,)), dma((33,)),
         dma((8,)), dma((8,)),
+        dma((5,)), dma((5,)),
     ]
     outs = pl.pallas_call(
         kernel,
@@ -715,18 +829,18 @@
             shape((TOK, TOK), BF16),
             shape((8, 1024), BF16),
             shape((8, 1024), BF16),
-            shape((8, TOK), F32),
-            shape((8, TOK), F32),
+            shape((heads, TOK), F32),
+            shape((heads, TOK), F32),
         ),
-        in_specs=[hbm, vm, hbm, vm, hbm] + [vm] * 8,
-        out_specs=(vm,) * 9,
+        in_specs=[hbm, vm, hbm, vm, hbm, vm, hbm, hbm, hbm, hbm, vm, vm] + [pl.BlockSpec(memory_space=pltpu.SMEM)],
+        out_specs=(hbm,) * 5 + (vm,) * 4,
         scratch_shapes=scratch,
         compiler_params=pltpu.CompilerParams(
             collective_id=0, has_side_effects=True, vmem_limit_bytes=67043328
         ),
         name="step",
     )(*args)
-    return outs[:7] + (outs[7][:heads], outs[8][:heads])
+    return hand_over(outs)
 
 
 def solution(mesh):

time: 201 us -> 152 us (0.76)
  Pallas kernels: 188 us -> 151 us
  local copies, waits for them, and re-layouts: 11.6 us -> 0 us
    pallas_call x1, Pallas kernels: 188 us -> 148 us  [shards(): pl.pallas_call(kernel, out_shape=(shape((512, 1024), BF16), shape((TOK, 1...]
    unnamed x31 -> x0, local copies, waits for them, and re-layouts: 8.48 us -> none
    pallas_call x0 -> x1, Pallas kernels: none -> 2.55 us  [hand_over(): pl.pallas_call(copy_kernel, out_shape=tuple((jax.ShapeDtypeStruct(a.shape...]
where the time goes in v2:
time: 152 us
  Pallas kernels  151 us (99%)
    pallas_call x1, Pallas kernels, shards(): pl.pallas_call(kernel, out_shape=(shape((512, 1024), BF16), shape((TOK, 1...  148 us

profile of v2, /device:TPU:1, one launch (start us, length us, event | category | flops | bytes accessed | tf_op | source)
XLA Modules:
  0.0 151.5 jit_solution(15060565621036995633)
XLA Ops:
  0.6 148.2 %step.1 = (bf16[512,1024]{1,0:T(8,128)(2,1)}, bf16[256,128]{1,0:T(8,128)(2,1)}, bf16[256,512]{1,0:T(8,128)(2,1)}, bf16[256,256]{1,0:T(8,128)(2,1)}, bf16[256,256...) custom-call(bf16[256,128]{1,0:T(8,128)(2,1)} %refs_0_.1, ...), custom_call_target="tpu_custom_call" | custom-call | tf_op jit(solution)/shard_map/step/pallas_call | solution.py:822
  148.8 2.5 %hand_over.1 = (bf16[512,1024]{1,0:T(8,128)(2,1)}, bf16[256,128]{1,0:T(8,128)(2,1)}, bf16[256,512]{1,0:T(8,128)(2,1)}, bf16[256,256]{1,0:T(8,128)(2,1)}, bf16[25...) custom-call(bf16[512,1024]{1,0:T(8,128)(2,1)} %get-tuple-element.18., ...), custom_call_target="tpu_custom_call" | custom-call | tf_op jit(solution)/shard_map/hand_over/pallas_call | solution.py:736

commit v3 on v2

--- a/solution.py
+++ b/solution.py
@@ -172,7 +172,7 @@
             copy.wait_send()
 
     def start(self):
-        for d in ORDER[1:]:
+        for d in (1, 7, 2, 6):
             ref = self.buf.at[self.v]
             send(ref, ref, self.s.at[0], self.r.at[d], {"vocab": self.x * 8 + (self.z + d) % 8})
 
@@ -180,6 +180,10 @@
         ref = self.buf.at[self.x * 8 + (self.z + 8 - d) % 8]
         if d:
             self.wait(ref, self.s.at[0], self.r.at[d], True)
+        if d in (2, 3):
+            send(ref, ref, self.s.at[0], self.r.at[d + 1], {"vocab": self.x * 8 + (self.z + 1) % 8})
+        if d == 6:
+            send(ref, ref, self.s.at[0], self.r.at[5], {"vocab": self.x * 8 + (self.z + 7) % 8})
         send(ref, ref, self.s.at[1], self.r.at[8 + d], {"vocab": self.xp * 8 + self.z})
         send(ref, ref, self.s.at[2], self.r.at[16 + d], {"vocab": self.xm * 8 + self.z})
 
@@ -194,10 +198,9 @@
         ref = self.buf.at[block, pl.ds(HALF, HALF)]
         send(ref, ref, self.s.at[4], self.r.at[32 + d], {"vocab": self.xm * 8 + self.z})
 
-    def spread(self, first=0):
-        for n in range(8):
-            if n >= first:
-                self.forward(ORDER[n])
+    def spread(self, first=0, stop=8):
+        for n in range(first, stop):
+            self.forward(ORDER[n])
             if n >= LAG:
                 self.pass_on(ORDER[n - LAG])
 
@@ -219,6 +222,60 @@
         self.wait(self.buf.at[pl.ds(0, 4)], self.s.at[4], self.r.at[0], False)
 
 
+class Swap:
+    def __init__(self, src, dst, rel, ssem, rsem, c):
+        self.src, self.dst, self.rel, self.s, self.r, self.c = src, dst, rel, ssem, rsem, c
+        y, self.k = c // 2, c % 2
+        self.at = lambda dy, kk: ((y + dy) % 4) * 2 + kk
+        self.top, self.bottom = pl.ds(0, TOK), pl.ds(TOK, TOK)
+
+    def copy(self, slot, arrive, src, dst, to):
+        return pltpu.make_async_remote_copy(
+            src_ref=src, dst_ref=dst, send_sem=self.s.at[slot], recv_sem=self.r.at[arrive],
+            device_id={"ctx": to}, device_id_type=MESH,
+        )
+
+    def sends(self):
+        c, k, at = self.c, self.k, self.at
+        first, second = [], []
+        for kk in range(2):
+            first.append((5 + kk, 5 + kk, self.src.at[at(2, kk), self.top], self.rel.at[kk], at(1, k)))
+            first.append((7 + kk, 7 + kk, self.src.at[at(2, kk), self.bottom], self.rel.at[2 + kk], at(3, k)))
+        for kk in range(2):
+            first.append((kk, k, self.src.at[at(1, kk)], self.dst.at[c], at(1, kk)))
+            first.append((2 + kk, 2 + k, self.src.at[at(3, kk)], self.dst.at[c], at(3, kk)))
+            second.append((9 + kk, 9 + k, self.rel.at[kk], self.dst.at[at(3, k), self.top], at(1, kk)))
+            second.append((11 + kk, 11 + k, self.rel.at[2 + kk], self.dst.at[at(1, k), self.bottom], at(3, kk)))
+        first.append((4, 4, self.src.at[at(0, 1 - k)], self.dst.at[c], at(0, 1 - k)))
+        return first, second
+
+    def start(self):
+        for args in self.sends()[0]:
+            self.copy(*args).start()
+
+    def got(self, arrive, ref):
+        self.copy(0, arrive, ref, ref, self.at(1, self.k)).wait_recv()
+
+    def forward(self):
+        for i in range(4):
+            self.got(5 + i, self.rel.at[i])
+        for args in self.sends()[1]:
+            self.copy(*args).start()
+
+    def finish(self):
+        for kk in range(2):
+            self.got(kk, self.dst.at[self.at(3, kk)])
+            self.got(2 + kk, self.dst.at[self.at(1, kk)])
+            self.got(9 + kk, self.dst.at[self.at(2, kk), self.top])
+            self.got(11 + kk, self.dst.at[self.at(2, kk), self.bottom])
+        self.got(4, self.dst.at[self.at(0, 1 - self.k)])
+
+    def drain(self):
+        first, second = self.sends()
+        for args in first + second:
+            self.copy(*args).wait_send()
+
+
 class Many:
     def __init__(self, axis, me, peer, count, src, dst, ssem, rsem):
         self.axis, self.me, self.peer, self.count = axis, me, peer, count
@@ -248,8 +305,8 @@
     (resid, gain, head_w, target, out_w, norm_gain, xs, gate, b_in, c_in, dt_in, decay_in, skip_in) = refs[:13]
     (gh_h, gr_h, gow_h, gx_h, gg_h, gb_o, gc_o, gdt_o, gld_o) = refs[13:22]
     (wbuf, owbuf, sbuf, nbuf, ntsend, ntbuf, logits, gall, pbuf, rel_a, rel_b, from_m, from_p, rz, gbuf,
-     ubuf, vbuf, osend, obuf, es, acc, lse_b, inner_b, gsum_b, gdot_b, mean_s, mean_b, b_send, b_got, c_send, c_got, orel, xs_v, gate_v, b_v, c_v, gh_o, gr_o, gow_o, gx_o, gg_o, mcol, ycur, cbb, cb_ch0, gyb,
-     lsem, ws, wr, ows, owr, gs, gr, us, ur, vs, vr, s1s, s1r, s2s, s2r, rs_s, rs_r, ms, mr, os_s, os_r) = refs[22:]
+     ubuf, vbuf, osend, obuf, es, acc, lse_b, inner_b, gsum_b, gdot_b, mean_s, mean_b, b_send, b_got, c_send, c_got, orel, nrel, xs_v, gate_v, b_v, c_v, gh_o, gr_o, gow_o, gx_o, gg_o, mcol, ycur, cbb, cb_ch0, gyb,
+     lsem, ws, wr, ows, owr, gs, gr, us, ur, vs, vr, s1s, s1r, s2s, s2r, rs_s, rs_r, ms, mr, os_s, os_r, nt_s, nt_r) = refs[22:]
     c = lax.axis_index("ctx")
     v = lax.axis_index("vocab")
     x, z = v // 8, v % 8
@@ -289,14 +346,13 @@
     stream = Voc(sbuf, s1s, s1r, v)
     back = Voc(gbuf, s2s, s2r, v)
     over_v = lambda d: (v + d) % VOC
-    over_c = lambda d: (c + d) % CTX
     quarter = (v // 4) * 4
     over_g = lambda d: quarter + (v % 4 + d) % 4
     lse_x = Many("vocab", v, over_v, VOC, lambda to: lse_b.at[v], lse_b, ms.at[0], mr.at[0])
     inner_x = Many("vocab", v, over_v, VOC, lambda to: inner_b.at[v], inner_b, ms.at[1], mr.at[1])
     gsum_x = Many("vocab", v, over_g, 4, lambda to: gsum_b.at[v % 4], gsum_b, ms.at[2], mr.at[2])
     gdot_x = Many("vocab", v, over_g, 4, lambda to: gdot_b.at[v % 4], gdot_b, ms.at[3], mr.at[3])
-    norm_x = Many("ctx", c, over_c, CTX, lambda to: ntsend.at[to], ntbuf, ms.at[4], mr.at[4])
+    norms = Swap(ntsend, ntbuf, nrel, nt_s, nt_r, c)
     b_x = Many("vocab", v, over_v, VOC, lambda to: b_send.at[to], b_got, ms.at[6], mr.at[6])
     c_x = Many("vocab", v, over_v, VOC, lambda to: c_send.at[to], c_got, ms.at[5], mr.at[5])
     mean_x = Many("vocab", v, over_v, VOC, lambda to: mean_s.at[to], mean_b, ms.at[7], mr.at[7])
@@ -460,15 +516,10 @@
 
     far, near = 1 - z // 4, z // 4
     serve = [4 * far + (z % 4 + 1 + j) % 4 for j in range(4)] + [4 * near + (z % 4 + 1 + j) % 4 for j in range(4)]
-    for n in range(8):
-        if n % 4 == 0:
-            partial(2 * x2 + (far, near)[n // 4])
-        rs_send(0, n, pbuf.at[x2 * 8 + serve[n], top], rel_a.at[n], to_p)
-        rs_send(1, n, pbuf.at[x2 * 8 + serve[n], bottom], rel_b.at[n], to_m)
-    grads.start()
-    for h in (far, near):
-        partial(2 * xp + h)
-        partial(2 * xm + h)
+    def first_relays(ns):
+        for n in ns:
+            rs_send(0, n, pbuf.at[x2 * 8 + serve[n], top], rel_a.at[n], to_p)
+            rs_send(1, n, pbuf.at[x2 * 8 + serve[n], bottom], rel_b.at[n], to_m)
 
     def relayed(n):
         rs_wait(0, n, rel_a.at[n])
@@ -480,19 +531,7 @@
         pbuf[i, HALF:TOK] = (pbuf[i, HALF:TOK].astype(F32) + rel_b[n].astype(F32)).astype(BF16)
         rs_send(3, n, pbuf.at[i], from_p.at[n], to_m)
 
-    for n in range(2):
-        relayed(n)
-    for h in (far, near):
-        partial(2 * x + h)
-    for n in range(2, 8):
-        relayed(n)
-    mean_b[v] = mean_s[v]
-    mean_x.start(v)
-    states.middle()
-    outs_w.middle()
-    norm_x.start(c)
-
-    for n in range(8):
+    def collect(n):
         rs_wait(2, n, from_m.at[n])
         rs_wait(3, n, from_p.at[n])
         i = x * 8 + serve[n]
@@ -500,9 +539,33 @@
         pbuf[i] = total.astype(BF16)
         if n < 7:
             send(pbuf.at[i], rz.at[z], rs_s.at[4], rs_r.at[32], {"vocab": i})
+
+    partial(2 * x2 + far)
+    first_relays(range(4))
+    partial(2 * xp + far)
+    partial(2 * xm + far)
+    for n in range(4):
+        relayed(n)
+    partial(2 * x2 + near)
+    first_relays(range(4, 8))
+    grads.start()
+    partial(2 * x + far)
+    partial(2 * xp + near)
+    partial(2 * xm + near)
+    partial(2 * x + near)
+    mean_b[v] = mean_s[v]
+    mean_x.start(v)
+    states.middle()
+    outs_w.middle()
+    norms.start()
+
+    for n in range(4):
+        collect(n)
+    for n in range(4, 8):
+        relayed(n)
+    for n in range(4, 8):
+        collect(n)
     rz[z] = pbuf[v]
-    states.end()
-    outs_w.end()
 
     inner_x.got()
     inner = column(jnp.sum(inner_b[...], axis=0)[0:1])
@@ -519,7 +582,12 @@
     puts[1].start()
     gbuf[v] = mine
     back.start()
-    back.forward(0)
+    back.spread(0, 5)
+    states.end()
+    outs_w.end()
+    back.spread(5, 8)
+    norms.forward()
+    back.relay()
     states.finish()
 
     def enter(j, h0):
@@ -539,16 +607,9 @@
     gsum_b[v % 4] = squares[0:1]
     gsum_x.start(v % 4)
 
-    back.spread(1)
-    back.relay()
-    gsum_x.got()
-    sums = jnp.sum(gsum_b[...], axis=0)
-    ginv = column(lax.rsqrt(sums * (1.0 / (INNER // GROUPS)) + EPS))
-    ginv = wide(ginv, TOK)
     ng = norm_gain[...]
-    normed_t = (gated * ginv * ng).astype(BF16).T
+    grads.middle()
     outs_w.finish()
-    grads.middle()
     back.finish()
 
     def project(i, total):
@@ -560,6 +621,11 @@
     dots = dot_high(jnp.ones((8, TOK), F32), gated * scaled, 1, 1)
     gdot_b[v % 4] = dots[0:1]
     gdot_x.start(v % 4)
+    gsum_x.got()
+    sums = jnp.sum(gsum_b[...], axis=0)
+    ginv = column(lax.rsqrt(sums * (1.0 / (INNER // GROUPS)) + EPS))
+    ginv = wide(ginv, TOK)
+    normed_t = (gated * ginv * ng).astype(BF16).T
 
     @pl.loop(0, CTX)
     def _(i):
@@ -609,14 +675,6 @@
                 if j == 2:
                     os_copies[1].start()
                     os_copies[2].start()
-            adjoints.middle()
-        if h == 3:
-            os_copies[1].wait_recv()
-            osend[at_p, top] = (osend[at_p, top].astype(F32) + orel[0].astype(F32)).astype(BF16)
-            os_copies[3].start()
-            os_copies[2].wait_recv()
-            osend[at_m, bottom] = (osend[at_m, bottom].astype(F32) + orel[1].astype(F32)).astype(BF16)
-            os_copies[4].start()
         pair = h // 2
         gyp = gyb[:, pair * 128 : pair * 128 + 128]
         gym = jnp.where(low if h % 2 == 0 else jnp.logical_not(low), gyp, 0.0)
@@ -632,8 +690,13 @@
             held = part
         else:
             logits[:, pair * 128 : pair * 128 + 128] = held + part
-    grads.end()
-    adjoints.end()
+    adjoints.middle()
+    os_copies[1].wait_recv()
+    osend[at_p, top] = (osend[at_p, top].astype(F32) + orel[0].astype(F32)).astype(BF16)
+    os_copies[3].start()
+    os_copies[2].wait_recv()
+    osend[at_m, bottom] = (osend[at_m, bottom].astype(F32) + orel[1].astype(F32)).astype(BF16)
+    os_copies[4].start()
     zero4 = jnp.zeros((4, TOK), F32)
     rows_m = jnp.concatenate(rows_m + [zero4], axis=0)
     cols_m = jnp.concatenate(cols_m + [zero4], axis=0)
@@ -643,16 +706,8 @@
     c_send[...] = dc.reshape(VOC, 8, 128).astype(BF16)
     c_x.start(v)
     c_got[v] = c_send[v]
-    grads.finish()
-    norm_x.got()
-    acc[...] = jnp.zeros_like(acc)
-
-    @pl.loop(0, CTX)
-    def _(i):
-        acc[...] += dot(ntbuf[i], gall[i])
-
-    gh_o[...] = acc[...].astype(BF16)
-    puts[0].start()
+    adjoints.end()
+    grads.end()
     adjoints.finish()
 
     def leave(j, h1):
@@ -681,6 +736,17 @@
     da = rows_m - cols_m + r_rows - wq
     at_end = cross + jnp.sum(wq, axis=1, keepdims=True)
     gld_o[...] = (dot_high(da, (row_i >= col_i).astype(F32)) + at_end)[0:4]
+
+    grads.finish()
+    norms.finish()
+    acc[...] = jnp.zeros_like(acc)
+
+    @pl.loop(0, CTX)
+    def _(i):
+        acc[...] += dot(ntbuf[i], gall[i])
+
+    gh_o[...] = acc[...].astype(BF16)
+    puts[0].start()
 
     os_copies[3].wait_recv()
     os_copies[4].wait_recv()
@@ -701,9 +767,10 @@
 
     for gather in (weights, outs_w, grads, states, adjoints):
         gather.drain()
+    norms.drain()
     stream.drain()
     back.drain()
-    for many in (lse_x, inner_x, gsum_x, gdot_x, norm_x, b_x, c_x, mean_x):
+    for many in (lse_x, inner_x, gsum_x, gdot_x, b_x, c_x, mean_x):
         many.drain()
     rs_wait(0, 0, rel_a, False)
     rs_wait(1, 0, rel_b, False)
@@ -798,6 +865,7 @@
         pltpu.VMEM((VOC, 8, 128), BF16),
         pltpu.VMEM((VOC, 8, 128), BF16),
         pltpu.VMEM((2, HALF, 512), BF16),
+        pltpu.VMEM((4, TOK, TOK), BF16),
         pltpu.VMEM((TOK, TOK), BF16),
         pltpu.VMEM((TOK, TOK), BF16),
         pltpu.VMEM((TOK, 128), BF16),
@@ -818,6 +886,7 @@
         dma((5,)), dma((33,)),
         dma((8,)), dma((8,)),
         dma((5,)), dma((5,)),
+        dma((13,)), dma((13,)),
     ]
     outs = pl.pallas_call(
         kernel,

time: 152 us -> 139 us (0.914)
  Pallas kernels: 151 us -> 138 us
    pallas_call x1, Pallas kernels: 148 us -> 135 us  [shards(): pl.pallas_call(kernel, out_shape=(shape((512, 1024), BF16), shape((TOK, 1...]
where the time goes in v3:
time: 139 us
  Pallas kernels  138 us (99%)
    pallas_call x1, Pallas kernels, shards(): pl.pallas_call(kernel, out_shape=(shape((512, 1024), BF16), shape((TOK, 1...  135 us

profile of v3, /device:TPU:1, one launch (start us, length us, event | category | flops | bytes accessed | tf_op | source)
XLA Modules:
  0.0 138.8 jit_solution(16375406221712218337)
XLA Ops:
  0.6 135.4 %step.1 = (bf16[512,1024]{1,0:T(8,128)(2,1)}, bf16[256,128]{1,0:T(8,128)(2,1)}, bf16[256,512]{1,0:T(8,128)(2,1)}, bf16[256,256]{1,0:T(8,128)(2,1)}, bf16[256,256...) custom-call(bf16[256,128]{1,0:T(8,128)(2,1)} %refs_0_.1, ...), custom_call_target="tpu_custom_call" | custom-call | tf_op jit(solution)/shard_map/step/pallas_call | solution.py:891
  136.0 2.5 %hand_over.1 = (bf16[512,1024]{1,0:T(8,128)(2,1)}, bf16[256,128]{1,0:T(8,128)(2,1)}, bf16[256,512]{1,0:T(8,128)(2,1)}, bf16[256,256]{1,0:T(8,128)(2,1)}, bf16[25...) custom-call(bf16[512,1024]{1,0:T(8,128)(2,1)} %get-tuple-element.18., ...), custom_call_target="tpu_custom_call" | custom-call | tf_op jit(solution)/shard_map/hand_over/pallas_call | solution.py:803

commit v4 on v3

--- a/solution.py
+++ b/solution.py
@@ -18,7 +18,7 @@
 VOC = 32
 TOK = 256
 HIGH = lax.Precision.HIGHEST
-STATE_ROWS = 160
+STATE_ROWS = 144
 HALF = TOK // 2
 
 
@@ -608,15 +608,17 @@
     gsum_x.start(v % 4)
 
     ng = norm_gain[...]
-    grads.middle()
     outs_w.finish()
-    back.finish()
-
-    def project(i, total):
+
+    def project(t, total):
+        i = (2 * x2 + 2 + t) % CTX
         lhs = jnp.concatenate([gbuf[4 * i + j] for j in range(4)], axis=1)
         return total + dot(lhs, owbuf[i], 1, 1)
 
-    grad_normed = lax.fori_loop(0, CTX, project, jnp.zeros((TOK, TOK), F32))
+    grad_normed = lax.fori_loop(0, 6, project, jnp.zeros((TOK, TOK), F32))
+    grads.middle()
+    back.finish()
+    grad_normed = lax.fori_loop(6, CTX, project, grad_normed)
     scaled = grad_normed * ng
     dots = dot_high(jnp.ones((8, TOK), F32), gated * scaled, 1, 1)
     gdot_b[v % 4] = dots[0:1]
@@ -660,7 +662,6 @@
     h0 = vbuf[c, 0:128]
     dc = dot_both(gye, h0, 1, 1)
     vbuf[c, 0:128] = dot_right(cc, gye, 0, 0)
-    vbuf[c, 128:STATE_ROWS] = jnp.zeros((STATE_ROWS - 128, TOK), F32)
     adjoints.start()
 
     ones8 = jnp.ones((8, TOK), F32)
@@ -669,12 +670,9 @@
     for h in range(4):
         if h == 2:
             os_copies[0].wait_recv()
-            for j in (2, 1, 3):
+            for j in range(1, 4):
                 i = k_at * 4 + (y_at + 4 - j) % 4
                 osend[i] = (osend[i].astype(F32) + obuf[(y_at + 4 - j) % 4].astype(F32)).astype(BF16)
-                if j == 2:
-                    os_copies[1].start()
-                    os_copies[2].start()
         pair = h // 2
         gyp = gyb[:, pair * 128 : pair * 128 + 128]
         gym = jnp.where(low if h % 2 == 0 else jnp.logical_not(low), gyp, 0.0)
@@ -691,12 +689,8 @@
         else:
             logits[:, pair * 128 : pair * 128 + 128] = held + part
     adjoints.middle()
-    os_copies[1].wait_recv()
-    osend[at_p, top] = (osend[at_p, top].astype(F32) + orel[0].astype(F32)).astype(BF16)
-    os_copies[3].start()
-    os_copies[2].wait_recv()
-    osend[at_m, bottom] = (osend[at_m, bottom].astype(F32) + orel[1].astype(F32)).astype(BF16)
-    os_copies[4].start()
+    os_copies[1].start()
+    os_copies[2].start()
     zero4 = jnp.zeros((4, TOK), F32)
     rows_m = jnp.concatenate(rows_m + [zero4], axis=0)
     cols_m = jnp.concatenate(cols_m + [zero4], axis=0)
@@ -707,8 +701,14 @@
     c_x.start(v)
     c_got[v] = c_send[v]
     adjoints.end()
+    os_copies[1].wait_recv()
+    osend[at_p, top] = (osend[at_p, top].astype(F32) + orel[0].astype(F32)).astype(BF16)
+    os_copies[3].start()
+    os_copies[2].wait_recv()
+    osend[at_m, bottom] = (osend[at_m, bottom].astype(F32) + orel[1].astype(F32)).astype(BF16)
+    os_copies[4].start()
+    adjoints.finish()
     grads.end()
-    adjoints.finish()
 
     def leave(j, h1):
         i = CTX - 1 - j
@@ -784,10 +784,15 @@
 
 
 def copy_kernel(*refs):
-    n = len(refs) // 3
+    n = (len(refs) - 2) // 3
     ins, outs, bufs, (sin, sout) = refs[:n], refs[n : 2 * n], refs[2 * n : 3 * n], refs[3 * n :]
-    loads = [pltpu.make_async_copy(ins[i], bufs[i], sin.at[i]) for i in range(n)]
-    stores = [pltpu.make_async_copy(bufs[i], outs[i], sout.at[i]) for i in range(n)]
+    parts = []
+    for i in range(n):
+        rows = ins[i].shape[0]
+        step = rows // 4 if rows >= 512 else rows
+        parts += [(i, pl.ds(r, step)) for r in range(0, rows, step)]
+    loads = [pltpu.make_async_copy(ins[i].at[r], bufs[i].at[r], sin.at[m]) for m, (i, r) in enumerate(parts)]
+    stores = [pltpu.make_async_copy(bufs[i].at[r], outs[i].at[r], sout.at[m]) for m, (i, r) in enumerate(parts)]
     for copy in loads:
         copy.start()
     for load, store in zip(loads, stores):
@@ -806,7 +811,7 @@
         in_specs=[hbm] * n,
         out_specs=(hbm,) * n,
         scratch_shapes=[pltpu.VMEM(a.shape, a.dtype) for a in arrays]
-        + [pltpu.SemaphoreType.DMA((n,)), pltpu.SemaphoreType.DMA((n,))],
+        + [pltpu.SemaphoreType.DMA((n + 3,)), pltpu.SemaphoreType.DMA((n + 3,))],
         name="hand_over",
     )(*arrays)
 
@@ -849,7 +854,7 @@
         pltpu.VMEM((8, TOK, 128), BF16),
         pltpu.VMEM((VOC, TOK, 128), BF16),
         pltpu.VMEM((CTX, STATE_ROWS, TOK), F32),
-        pltpu.VMEM((CTX, STATE_ROWS, TOK), F32),
+        pltpu.VMEM((CTX, 128, TOK), F32),
         pltpu.VMEM((CTX, TOK, 512), BF16),
         pltpu.VMEM((CTX, TOK, 512), BF16),
         pltpu.VMEM((4, TOK, TOK), F32),

time: 139 us -> 136 us (0.978)
  Pallas kernels: 138 us -> 135 us
    pallas_call x1, Pallas kernels: 135 us -> 132 us  [shards(): pl.pallas_call(kernel, out_shape=(shape((512, 1024), BF16), shape((TOK, 1...]
where the time goes in v4:
time: 136 us; the launch traced here: 135 us
  Pallas kernels  135 us (99%)
    pallas_call x1, Pallas kernels, shards(): pl.pallas_call(kernel, out_shape=(shape((512, 1024), BF16), shape((TOK, 1...  132 us

profile of v4, /device:TPU:1, one launch (start us, length us, event | category | flops | bytes accessed | tf_op | source)
XLA Modules:
  0.0 135.4 jit_solution(11526745823737732591)
XLA Ops:
  0.6 132.3 %step.1 = (bf16[512,1024]{1,0:T(8,128)(2,1)}, bf16[256,128]{1,0:T(8,128)(2,1)}, bf16[256,512]{1,0:T(8,128)(2,1)}, bf16[256,256]{1,0:T(8,128)(2,1)}, bf16[256,256...) custom-call(bf16[256,128]{1,0:T(8,128)(2,1)} %refs_0_.1, ...), custom_call_target="tpu_custom_call" | custom-call | tf_op jit(solution)/shard_map/step/pallas_call | solution.py:896
  132.9 2.3 %hand_over.1 = (bf16[512,1024]{1,0:T(8,128)(2,1)}, bf16[256,128]{1,0:T(8,128)(2,1)}, bf16[256,512]{1,0:T(8,128)(2,1)}, bf16[256,256]{1,0:T(8,128)(2,1)}, bf16[25...) custom-call(bf16[512,1024]{1,0:T(8,128)(2,1)} %get-tuple-element.18., ...), custom_call_target="tpu_custom_call" | custom-call | tf_op jit(solution)/shard_map/hand_over/pallas_call | solution.py:808
